TPU v7x, 32 devices: a whole 2x2x4 slice. The times are simulated.
32 devices in a mesh: rep: 2 (over x), fsdp: 16 (over z, y, core).
Axes of the slice: x: 2, y: 2, z: 4, core: 2. Of those that a mesh axis runs over, the one named last changes fastest.
Arguments:
- prompt_rows: bfloat16 [8192, 1024], P(('rep', 'fsdp')), may hold values from -12 to 12
- suffix_rows: bfloat16 [8192, 1024], P(('rep', 'fsdp')), may hold values from -12 to 12
- assignment: int32 [2, 32], P('rep', 'fsdp'), may hold values from 0 to 31, each once within a row
- lengths: int32 [2, 32], P('rep', 'fsdp'), may hold values from 1 to 128, 3072 in all within a row
- attention_gain: bfloat16 [1024], P('fsdp'), may hold values from 0.5 to 1.5
- query_weight: bfloat16 [1024, 2048], P('fsdp'), may hold values from -0.1875 to 0.1875
- key_matrix: bfloat16 [1024, 1024], P('fsdp'), may hold values from -0.1875 to 0.1875
- value_matrix: bfloat16 [1024, 1024], P('fsdp'), may hold values from -0.1875 to 0.1875
- query_gain: bfloat16 [128], P('fsdp'), may hold values from 0.5 to 1.5
- key_norm_gain: bfloat16 [128], P('fsdp'), may hold values from 0.5 to 1.5
- out_weight: bfloat16 [2048, 1024], P('fsdp'), may hold values from -2 to 2
- mlp_gain: bfloat16 [1024], P('fsdp'), may hold values from 0.5 to 1.5
- gate_weight: bfloat16 [1024, 3072], P('fsdp'), may hold values from -0.1875 to 0.1875
- up_weight: bfloat16 [1024, 3072], P('fsdp'), may hold values from -0.1875 to 0.1875
- down_weight: bfloat16 [3072, 1024], P('fsdp'), may hold values from -0.109375 to 0.109375
- prompt_cotangent: bfloat16 [8192, 1024], P(('rep', 'fsdp')), may hold values from -18 to 18
- suffix_cotangent: bfloat16 [8192, 1024], P(('rep', 'fsdp')), may hold values from -18 to 18
Outputs:
- prompt_mixed: bfloat16 [8192, 1024], P(('rep', 'fsdp'))
- suffix_mixed: bfloat16 [8192, 1024], P(('rep', 'fsdp'))
- prompt_grad: float32 [8192, 1024], P(('rep', 'fsdp'))
- suffix_grad: float32 [8192, 1024], P(('rep', 'fsdp'))
- grad_attention_gain: float32 [1024], P('fsdp')
- grad_query_weight: float32 [1024, 2048], P('fsdp')
- grad_key_weight: float32 [1024, 1024], P('fsdp')
- grad_value_weight: float32 [1024, 1024], P('fsdp')
- grad_query_gain: float32 [128], P('fsdp')
- grad_key_gain: float32 [128], P('fsdp')
- grad_out_weight: float32 [2048, 1024], P('fsdp')
- grad_mlp_gain: float32 [1024], P('fsdp')
- grad_gate_weight: float32 [1024, 3072], P('fsdp')
- grad_up_weight: float32 [1024, 3072], P('fsdp')
- grad_down_weight: float32 [3072, 1024], P('fsdp')
- token_norms: float32 [3], replicated
Inputs may be any that keep to these rules, and one draw needn't show every extreme that they name: Each row of assignment is a permutation; so every prompt has exactly 8 continuation slots. Each row of lengths sums to 3072 and holds 128 at least once.
All inputs are finite; a program needn't handle non-finite values. No bound on the sum of `lengths` on one device may be relied on, other than what follows from the above.
Results may differ from a plain program's by a relative error of at most 0.024.
Values may be sent and summed in bfloat16 or wider, within the bound.
A program may use at most 256 MiB of HBM per device.

v0:
```python
from functools import partial

import jax
import jax.numpy as jnp
from jax import lax
from jax.sharding import PartitionSpec as P

MODEL_WIDTH = 1024
QUERY_HEADS = 16
KEY_VALUE_HEADS = 8
HEAD_SIZE = 128
PROMPT_LENGTH = 1024
CONT = 8
CONTINUATION_LEN = 128


norm_epsilon = 1e-06
rope_theta = 1000000.0
masked_score = -1e30


def as_sent(shard):
    return jax.tree.map(lambda a: a.astype(jnp.bfloat16) if a.dtype == jnp.float32 else a, shard)


def root_mean_scale(values, gain_vector):
    return (
        values
        * lax.rsqrt(jnp.mean(values * values, axis=-1, keepdims=True) + norm_epsilon)
        * gain_vector
    )


def rotary_embed(values, token_positions):
    half_size = values.shape[-1] // 2
    inverse = rope_theta ** (jnp.arange(half_size, dtype=jnp.float32) * (-2.0 / values.shape[-1]))
    angles = token_positions.astype(jnp.float32)[:, None] * inverse[None, :]
    cosine = jnp.cos(angles)[:, None, :]
    sine_part = jnp.sin(angles)[:, None, :]
    first_half = values[..., :half_size]
    second_half = values[..., half_size:]
    return jnp.concatenate(
        [
            first_half * cosine - second_half * sine_part,
            second_half * cosine + first_half * sine_part,
        ],
        axis=-1,
    )


def query_key(token_positions, query_pre, key_before_norm, query_scale, key_norm_scale):
    count_of_rows = query_pre.shape[0]
    query_rotated = rotary_embed(
        root_mean_scale(query_pre.reshape(count_of_rows, QUERY_HEADS, HEAD_SIZE), query_scale),
        token_positions,
    )
    key_rotated = rotary_embed(
        root_mean_scale(
            key_before_norm.reshape(count_of_rows, KEY_VALUE_HEADS, HEAD_SIZE), key_norm_scale
        ),
        token_positions,
    )
    return (query_rotated, key_rotated)


def swiglu(gate_pre, up_pre):
    return jax.nn.silu(gate_pre) * up_pre


def unit_scores(grouped_query, key_block):
    return jnp.einsum(
        "rhgd,khd->hgrk", grouped_query, key_block, preferred_element_type=jnp.float32
    ) * HEAD_SIZE ** (-0.5)


def unit_forward(grouped_query, key_block, value_block, allowed):
    scores = unit_scores(grouped_query, key_block)
    masked = jnp.where(allowed, scores, masked_score)
    top_score = jnp.max(masked, axis=-1)
    total = jnp.sum(jnp.where(allowed, jnp.exp(masked - top_score[..., None]), 0.0), axis=-1)
    log_total = top_score + jnp.log(total)
    probs_low = jnp.where(allowed, jnp.exp(scores - log_total[..., None]), 0.0).astype(jnp.bfloat16)
    result = jnp.einsum(
        "hgrk,khd->rhgd", probs_low, value_block, preferred_element_type=jnp.float32
    )
    return (result, log_total)


def unit_backward(
    grouped_query,
    key_block,
    value_block,
    allowed,
    log_total,
    grad_attended_per_group,
    row_difference,
):
    scores = unit_scores(grouped_query, key_block)
    probs_wide = jnp.where(allowed, jnp.exp(scores - log_total[..., None]), 0.0)
    probs_low = probs_wide.astype(jnp.bfloat16)
    d_value_block = jnp.einsum(
        "hgrk,rhgd->khd", probs_low, grad_attended_per_group, preferred_element_type=jnp.float32
    )
    d_probs = jnp.einsum(
        "rhgd,khd->hgrk", grad_attended_per_group, value_block, preferred_element_type=jnp.float32
    )
    d_scores = (probs_wide * (d_probs - row_difference[..., None])).astype(jnp.bfloat16)
    d_query = jnp.einsum(
        "hgrk,khd->rhgd", d_scores, key_block, preferred_element_type=jnp.float32
    ) * HEAD_SIZE ** (-0.5)
    d_key_block = jnp.einsum(
        "hgrk,rhgd->khd", d_scores, grouped_query, preferred_element_type=jnp.float32
    ) * HEAD_SIZE ** (-0.5)
    return (d_query, d_key_block, d_value_block)


def per_device(
    prompt_rows,
    suffix_rows,
    assignment,
    lengths,
    attention_gain,
    query_weight,
    key_matrix,
    value_matrix,
    query_gain,
    key_norm_gain,
    out_weight,
    mlp_gain,
    gate_weight,
    up_weight,
    down_weight,
    prompt_cotangent,
    suffix_cotangent,
):
    fsdp_rank = lax.axis_index("fsdp")
    prompt_on_device = prompt_rows.shape[0]
    continuation_on_device = suffix_rows.shape[0]
    device_slots = continuation_on_device // CONTINUATION_LEN
    number_of_rows = prompt_on_device + continuation_on_device
    heads_per_group = QUERY_HEADS // KEY_VALUE_HEADS
    first_row = fsdp_rank * prompt_on_device
    owned_group = first_row // PROMPT_LENGTH
    prompt_place = first_row % PROMPT_LENGTH + jnp.arange(prompt_on_device, dtype=jnp.int32)
    suffix_place = jnp.arange(continuation_on_device, dtype=jnp.int32) % CONTINUATION_LEN
    owner_slots = assignment[0] // CONT
    length_rows = jnp.repeat(lengths[0], CONTINUATION_LEN)
    suffix_valid = suffix_place < length_rows
    slot_validity = suffix_valid.reshape(device_slots, CONTINUATION_LEN)
    token_positions = jnp.concatenate([prompt_place, PROMPT_LENGTH + suffix_place])
    valid_rows = jnp.concatenate(
        [jnp.ones((prompt_on_device,), jnp.float32), suffix_valid.astype(jnp.float32)]
    )
    prompt_allowed = jnp.arange(PROMPT_LENGTH, dtype=jnp.int32)[None, :] <= prompt_place[:, None]
    slot_causal = (
        jnp.arange(CONTINUATION_LEN, dtype=jnp.int32)[None, :]
        <= jnp.arange(CONTINUATION_LEN, dtype=jnp.int32)[:, None]
    )

    def slot_allowed(valid_slot):
        return jnp.concatenate(
            [
                jnp.ones((CONTINUATION_LEN, PROMPT_LENGTH), dtype=bool),
                slot_causal & valid_slot[None, :],
            ],
            axis=1,
        )

    attention_set = (
        lax.all_gather(attention_gain, "fsdp", axis=0, tiled=True),
        lax.all_gather(query_weight, "fsdp", axis=0, tiled=True),
        lax.all_gather(key_matrix, "fsdp", axis=0, tiled=True),
        lax.all_gather(value_matrix, "fsdp", axis=0, tiled=True),
        lax.all_gather(query_gain, "fsdp", axis=0, tiled=True),
        lax.all_gather(key_norm_gain, "fsdp", axis=0, tiled=True),
        lax.all_gather(out_weight, "fsdp", axis=0, tiled=True),
    )
    gain_first, query_full, key_full, value_full, query_scale, key_norm_scale, out_full = (
        attention_set
    )
    rows_wide = jnp.concatenate([prompt_rows, suffix_rows], 0).astype(jnp.float32)
    hidden_wide, first_pull = jax.vjp(root_mean_scale, rows_wide, gain_first.astype(jnp.float32))
    hidden_state = hidden_wide.astype(jnp.bfloat16)
    query_pre = jnp.dot(hidden_state, query_full, preferred_element_type=jnp.float32)
    key_before_norm = jnp.dot(hidden_state, key_full, preferred_element_type=jnp.float32)
    value_matrix_rows = (
        jnp.dot(hidden_state, value_full, preferred_element_type=jnp.float32)
        .astype(jnp.bfloat16)
        .reshape(number_of_rows, KEY_VALUE_HEADS, HEAD_SIZE)
    )
    (query_rotated, key_rotated), rotary_pull = jax.vjp(
        partial(query_key, token_positions),
        query_pre,
        key_before_norm,
        query_scale.astype(jnp.float32),
        key_norm_scale.astype(jnp.float32),
    )
    grouped_query = query_rotated.astype(jnp.bfloat16).reshape(
        number_of_rows, KEY_VALUE_HEADS, heads_per_group, HEAD_SIZE
    )
    key_reduced = key_rotated.astype(jnp.bfloat16)
    gathered_keys, gathered_values = (
        lax.all_gather(key_reduced[:prompt_on_device], "fsdp", axis=0, tiled=True),
        lax.all_gather(value_matrix_rows[:prompt_on_device], "fsdp", axis=0, tiled=True),
    )
    prompt_count = gathered_keys.shape[0]
    prompt_query = grouped_query[:prompt_on_device]
    own_prompt_keys = lax.dynamic_slice_in_dim(
        gathered_keys, owned_group * PROMPT_LENGTH, PROMPT_LENGTH, 0
    )
    own_prompt_values = lax.dynamic_slice_in_dim(
        gathered_values, owned_group * PROMPT_LENGTH, PROMPT_LENGTH, 0
    )
    slot_query_rows = grouped_query[prompt_on_device:].reshape(
        device_slots, CONTINUATION_LEN, KEY_VALUE_HEADS, heads_per_group, HEAD_SIZE
    )
    slot_key_rows = key_reduced[prompt_on_device:].reshape(
        device_slots, CONTINUATION_LEN, KEY_VALUE_HEADS, HEAD_SIZE
    )
    slot_value_rows = value_matrix_rows[prompt_on_device:].reshape(
        device_slots, CONTINUATION_LEN, KEY_VALUE_HEADS, HEAD_SIZE
    )

    def slot_keys_of(owner, own_keys, own_values):
        keys_all = jnp.concatenate(
            [
                lax.dynamic_slice_in_dim(gathered_keys, owner * PROMPT_LENGTH, PROMPT_LENGTH, 0),
                own_keys,
            ],
            0,
        )
        values_all = jnp.concatenate(
            [
                lax.dynamic_slice_in_dim(gathered_values, owner * PROMPT_LENGTH, PROMPT_LENGTH, 0),
                own_values,
            ],
            0,
        )
        return (keys_all, values_all)

    prompt_output, prompt_lse = unit_forward(
        prompt_query, own_prompt_keys, own_prompt_values, prompt_allowed
    )

    def slot_forward(slot_items):
        query_slot, own_keys, own_values, owner, valid_slot = slot_items
        keys_all, values_all = slot_keys_of(owner, own_keys, own_values)
        return unit_forward(query_slot, keys_all, values_all, slot_allowed(valid_slot))

    slot_output, slot_lse = lax.map(
        slot_forward, (slot_query_rows, slot_key_rows, slot_value_rows, owner_slots, slot_validity)
    )
    attended_group = jnp.concatenate(
        [
            prompt_output,
            slot_output.reshape(
                continuation_on_device, KEY_VALUE_HEADS, heads_per_group, HEAD_SIZE
            ),
        ],
        0,
    )
    attended = attended_group.reshape(number_of_rows, QUERY_HEADS * HEAD_SIZE)
    attended_low = attended.astype(jnp.bfloat16)
    residual = rows_wide + jnp.dot(attended_low, out_full, preferred_element_type=jnp.float32)
    mlp_set = (
        lax.all_gather(mlp_gain, "fsdp", axis=0, tiled=True),
        lax.all_gather(gate_weight, "fsdp", axis=0, tiled=True),
        lax.all_gather(up_weight, "fsdp", axis=0, tiled=True),
        lax.all_gather(down_weight, "fsdp", axis=0, tiled=True),
    )
    gain_second, gate_full, up_full, down_full = mlp_set
    hidden_two_wide, second_pull = jax.vjp(
        root_mean_scale, residual, gain_second.astype(jnp.float32)
    )
    hidden_two = hidden_two_wide.astype(jnp.bfloat16)
    gate_pre = jnp.dot(hidden_two, gate_full, preferred_element_type=jnp.float32)
    up_pre = jnp.dot(hidden_two, up_full, preferred_element_type=jnp.float32)
    act_wide, act_pull = jax.vjp(swiglu, gate_pre, up_pre)
    act_low = act_wide.astype(jnp.bfloat16)
    mixed_full = residual + jnp.dot(act_low, down_full, preferred_element_type=jnp.float32)
    gate_back, up_back, down_back = (
        lax.all_gather(gate_weight, "fsdp", axis=0, tiled=True),
        lax.all_gather(up_weight, "fsdp", axis=0, tiled=True),
        lax.all_gather(down_weight, "fsdp", axis=0, tiled=True),
    )
    d_mixed = (
        jnp.concatenate([prompt_cotangent, suffix_cotangent], 0).astype(jnp.float32)
        * valid_rows[:, None]
    )
    d_mixed_low = d_mixed.astype(jnp.bfloat16)
    grad_down = jnp.einsum("rf,rd->fd", act_low, d_mixed_low, preferred_element_type=jnp.float32)
    d_act = jnp.einsum("rd,fd->rf", d_mixed_low, down_back, preferred_element_type=jnp.float32)
    d_gate_wide, d_up_wide = act_pull(d_act)
    d_gate = d_gate_wide.astype(jnp.bfloat16)
    d_up = d_up_wide.astype(jnp.bfloat16)
    grad_gate = jnp.einsum("rd,rf->df", hidden_two, d_gate, preferred_element_type=jnp.float32)
    grad_up = jnp.einsum("rd,rf->df", hidden_two, d_up, preferred_element_type=jnp.float32)
    d_hidden_two = jnp.einsum(
        "rf,df->rd", d_gate, gate_back, preferred_element_type=jnp.float32
    ) + jnp.einsum("rf,df->rd", d_up, up_back, preferred_element_type=jnp.float32)
    d_resid_mlp, grad_second_gain = second_pull(d_hidden_two)
    d_resid = d_mixed + d_resid_mlp
    mlp_shards = (
        lax.psum_scatter(
            grad_second_gain.astype(jnp.bfloat16), "fsdp", scatter_dimension=0, tiled=True
        ).astype(jnp.float32),
        lax.psum_scatter(
            grad_gate.astype(jnp.bfloat16), "fsdp", scatter_dimension=0, tiled=True
        ).astype(jnp.float32),
        lax.psum_scatter(
            grad_up.astype(jnp.bfloat16), "fsdp", scatter_dimension=0, tiled=True
        ).astype(jnp.float32),
        lax.psum_scatter(
            grad_down.astype(jnp.bfloat16), "fsdp", scatter_dimension=0, tiled=True
        ).astype(jnp.float32),
    )
    query_back, key_back, value_back, out_back = (
        lax.all_gather(query_weight, "fsdp", axis=0, tiled=True),
        lax.all_gather(key_matrix, "fsdp", axis=0, tiled=True),
        lax.all_gather(value_matrix, "fsdp", axis=0, tiled=True),
        lax.all_gather(out_weight, "fsdp", axis=0, tiled=True),
    )
    d_resid_low = d_resid.astype(jnp.bfloat16)
    grad_out = jnp.einsum(
        "ra,rd->ad", attended_low, d_resid_low, preferred_element_type=jnp.float32
    )
    grad_attended_rows = jnp.einsum(
        "rd,ad->ra", d_resid_low, out_back, preferred_element_type=jnp.float32
    ).astype(jnp.bfloat16)
    grad_attended_per_group = grad_attended_rows.reshape(
        number_of_rows, KEY_VALUE_HEADS, heads_per_group, HEAD_SIZE
    )
    row_difference = jnp.einsum(
        "rhgd,rhgd->hgr", grad_attended_per_group.astype(jnp.float32), attended_group
    )
    grad_prompt_query, grad_prompt_keys, grad_prompt_values = unit_backward(
        prompt_query,
        own_prompt_keys,
        own_prompt_values,
        prompt_allowed,
        prompt_lse,
        grad_attended_per_group[:prompt_on_device],
        row_difference[..., :prompt_on_device],
    )
    key_buffer = lax.dynamic_update_slice_in_dim(
        jnp.zeros((prompt_count, KEY_VALUE_HEADS, HEAD_SIZE), jnp.float32),
        grad_prompt_keys,
        owned_group * PROMPT_LENGTH,
        0,
    )
    value_buffer = lax.dynamic_update_slice_in_dim(
        jnp.zeros((prompt_count, KEY_VALUE_HEADS, HEAD_SIZE), jnp.float32),
        grad_prompt_values,
        owned_group * PROMPT_LENGTH,
        0,
    )
    slot_d_attended = grad_attended_per_group[prompt_on_device:].reshape(
        device_slots, CONTINUATION_LEN, KEY_VALUE_HEADS, heads_per_group, HEAD_SIZE
    )
    slot_delta = jnp.moveaxis(
        row_difference[..., prompt_on_device:].reshape(
            KEY_VALUE_HEADS, heads_per_group, device_slots, CONTINUATION_LEN
        ),
        2,
        0,
    )

    def slot_backward(buffers, slot_items):
        query_slot, own_keys, own_values, owner, valid_slot, lse_slot, d_att_slot, delta_slot = (
            slot_items
        )
        keys_all, values_all = slot_keys_of(owner, own_keys, own_values)
        d_query_slot, d_keys_all, d_values_all = unit_backward(
            query_slot,
            keys_all,
            values_all,
            slot_allowed(valid_slot),
            lse_slot,
            d_att_slot,
            delta_slot,
        )
        key_acc, value_acc = buffers
        start = owner * PROMPT_LENGTH
        key_acc = lax.dynamic_update_slice_in_dim(
            key_acc,
            lax.dynamic_slice_in_dim(key_acc, start, PROMPT_LENGTH, 0) + d_keys_all[:PROMPT_LENGTH],
            start,
            0,
        )
        value_acc = lax.dynamic_update_slice_in_dim(
            value_acc,
            lax.dynamic_slice_in_dim(value_acc, start, PROMPT_LENGTH, 0)
            + d_values_all[:PROMPT_LENGTH],
            start,
            0,
        )
        return (
            (key_acc, value_acc),
            (d_query_slot, d_keys_all[PROMPT_LENGTH:], d_values_all[PROMPT_LENGTH:]),
        )

    (key_buffer, value_buffer), (grad_slot_queries, owned_key_grads, owned_value_grads) = lax.scan(
        slot_backward,
        (key_buffer, value_buffer),
        (
            slot_query_rows,
            slot_key_rows,
            slot_value_rows,
            owner_slots,
            slot_validity,
            slot_lse,
            slot_d_attended,
            slot_delta,
        ),
    )
    owned_keys, owned_values = (
        lax.psum_scatter(
            key_buffer.astype(jnp.bfloat16), "fsdp", scatter_dimension=0, tiled=True
        ).astype(jnp.float32),
        lax.psum_scatter(
            value_buffer.astype(jnp.bfloat16), "fsdp", scatter_dimension=0, tiled=True
        ).astype(jnp.float32),
    )
    d_query = jnp.concatenate(
        [
            grad_prompt_query,
            grad_slot_queries.reshape(
                continuation_on_device, KEY_VALUE_HEADS, heads_per_group, HEAD_SIZE
            ),
        ],
        0,
    )
    grad_key_rotated = jnp.concatenate(
        [owned_keys, owned_key_grads.reshape(continuation_on_device, KEY_VALUE_HEADS, HEAD_SIZE)], 0
    )
    d_values_low = (
        jnp.concatenate(
            [
                owned_values,
                owned_value_grads.reshape(continuation_on_device, KEY_VALUE_HEADS, HEAD_SIZE),
            ],
            0,
        )
        .astype(jnp.bfloat16)
        .reshape(number_of_rows, KEY_VALUE_HEADS * HEAD_SIZE)
    )
    d_query_pre, d_key_pre, grad_query_scale, grad_key_scale = rotary_pull(
        (d_query.reshape(number_of_rows, QUERY_HEADS, HEAD_SIZE), grad_key_rotated)
    )
    d_query_low = d_query_pre.astype(jnp.bfloat16)
    d_key_low = d_key_pre.astype(jnp.bfloat16)
    grad_query = jnp.einsum(
        "rd,rq->dq", hidden_state, d_query_low, preferred_element_type=jnp.float32
    )
    grad_key = jnp.einsum("rd,rq->dq", hidden_state, d_key_low, preferred_element_type=jnp.float32)
    grad_value = jnp.einsum(
        "rd,rq->dq", hidden_state, d_values_low, preferred_element_type=jnp.float32
    )
    d_hidden = (
        jnp.einsum("rq,dq->rd", d_query_low, query_back, preferred_element_type=jnp.float32)
        + jnp.einsum("rq,dq->rd", d_key_low, key_back, preferred_element_type=jnp.float32)
        + jnp.einsum("rq,dq->rd", d_values_low, value_back, preferred_element_type=jnp.float32)
    )
    d_rows_attn, grad_first_gain = first_pull(d_hidden)
    d_rows = d_resid + d_rows_attn
    stats = jnp.stack(
        [
            jnp.sum(valid_rows * jnp.sum(mixed_full * mixed_full, axis=-1)),
            jnp.sum(valid_rows * jnp.sum(residual * residual, axis=-1)),
            jnp.sum(valid_rows * jnp.sum(d_rows * d_rows, axis=-1)),
            jnp.sum(valid_rows),
        ]
    )
    stat_extra = ()
    attention_shards = jax.tree.map(
        lambda part: part.astype(jnp.float32),
        lax.psum_scatter(
            as_sent(
                (
                    grad_first_gain,
                    grad_query,
                    grad_key,
                    grad_value,
                    grad_query_scale,
                    grad_key_scale,
                    grad_out,
                )
                + stat_extra
            ),
            "fsdp",
            scatter_dimension=0,
            tiled=True,
        ),
    )
    summed = jax.tree.map(
        lambda part: part.astype(jnp.float32),
        lax.psum(as_sent(attention_shards + mlp_shards), "rep"),
    )
    stat_sums = lax.psum(stats, ("rep", "fsdp"))
    token_norms = jnp.sqrt(stat_sums[:3] / (stat_sums[3] * MODEL_WIDTH))
    mixed_low = mixed_full.astype(jnp.bfloat16)
    mlp_done = summed[-4:]
    return (
        mixed_low[:prompt_on_device],
        mixed_low[prompt_on_device:],
        d_rows[:prompt_on_device],
        d_rows[prompt_on_device:],
        summed[0],
        summed[1],
        summed[2],
        summed[3],
        summed[4],
        summed[5],
        summed[6],
        mlp_done[0],
        mlp_done[1],
        mlp_done[2],
        mlp_done[3],
        token_norms,
    )


def solution(mesh):
    placed = (
        P(("rep", "fsdp"), None),
        P(("rep", "fsdp"), None),
        P("rep", "fsdp"),
        P("rep", "fsdp"),
        P("fsdp"),
        P("fsdp", None),
        P("fsdp", None),
        P("fsdp", None),
        P("fsdp"),
        P("fsdp"),
        P("fsdp", None),
        P("fsdp"),
        P("fsdp", None),
        P("fsdp", None),
        P("fsdp", None),
        P(("rep", "fsdp"), None),
        P(("rep", "fsdp"), None),
    )
    return jax.shard_map(
        per_device,
        mesh=mesh,
        in_specs=placed,
        out_specs=(
            P(("rep", "fsdp"), None),
            P(("rep", "fsdp"), None),
            P(("rep", "fsdp"), None),
            P(("rep", "fsdp"), None),
            P("fsdp"),
            P("fsdp", None),
            P("fsdp", None),
            P("fsdp", None),
            P("fsdp"),
            P("fsdp"),
            P("fsdp", None),
            P("fsdp"),
            P("fsdp", None),
            P("fsdp", None),
            P("fsdp", None),
            P(),
        ),
        check_vma=False,
    )
```

profile of v0, /device:TPU:0, one launch (start us, length us, event | category | flops | bytes accessed | tf_op | source)
XLA Modules:
  0.0 1619.7 jit_solution(15310374002987934982)
XLA Ops:
  15.5 35.8 %all-reduce.16 = (bf16[1024]{0:T(1024)(128)(2,1)S(1)}, bf16[128]{0:T(256)(128)(2,1)S(1)}, bf16[128]{0:T(256)(128)(2,1)S(1)}, bf16[1024]{0:T(1024)(128)(2,1)S(1)}) all-reduce(bf16[1024]{0:T(1024)(128)(2,1)S(1)} %dynamic-update-slice, bf16[128]{0:T(256)(128)(2,1)S(1)} %dynamic-update-slice.1, ...), channel_id=1, replica_groups=mesh['rep'=2,'fsdp'=16] {'fsdp'}, use_global_device_ids=true, to_apply=%add.7 | all-reduce | flops 2304 | bytes 9216
  60.7 36.0 %all-gather.14.cloned.1.call-done = bf16[1024,1024]{1,0:T(8,128)(2,1)} async-done(((bf16[64,1024]{1,0:T(8,128)(2,1)}), bf16[1024,1024]{1,0:T(8,128)(2,1)}) %all-gather.14.cloned.1.call-update) | async-done | bytes 2097168 | tf_op jit(solution)/shard_map/all_gather | solution.py:172
  109.1 39.4 %all-gather.18.cloned.1.call-done = bf16[1024,2048]{1,0:T(8,128)(2,1)} async-done(((bf16[64,2048]{1,0:T(8,128)(2,1)}), bf16[1024,2048]{1,0:T(8,128)(2,1)}) %all-gather.18.cloned.1.call-update) | async-done | bytes 4194320 | tf_op jit(solution)/shard_map/all_gather | solution.py:171
  164.0 63.7 %all-gather.12.cloned.1.call-done = bf16[4096,8,128]{0,2,1:T(8,128)(2,1)} async-done(((bf16[256,8,128]{0,2,1:T(8,128)(2,1)}), bf16[4096,8,128]{0,2,1:T(8,128)(2,1)}) %all-gather.12.cloned.1.call-update) | async-done | bytes 8388624 | tf_op jit(solution)/shard_map/all_gather | solution.py:204
  227.6 75.7 %all-gather.16.cloned.1.call-done = bf16[4096,8,128]{2,0,1:T(8,128)(2,1)} async-done(((bf16[256,8,128]{2,0,1:T(8,128)(2,1)}), bf16[4096,8,128]{2,0,1:T(8,128)(2,1)}) %all-gather.16.cloned.1.call-update) | async-done | bytes 8388624 | tf_op jit(solution)/shard_map/all_gather | solution.py:203
  303.4 24.6 %while.32 = (s32[]{:T(128)}, f32[2,128,8,2,128]{1,4,3,2,0:T(8,128)}, f32[2,8,2,128]{3,2,1,0:T(2,128)S(1)}, s32[2]{0:T(128)S(1)}, bf16[4096,8,128]{0,2,1:T(8,128)...) while((s32[]{:T(128)}, ...), condition=%wide.region_8.9_spmd.clone, body=%wide.region_5.8_spmd.clone.sunk | while | flops 1245739008 | bytes 66224836 | solution.py:250
  364.8 52.2 %all-gather.24.cloned.1.call-done = bf16[1024,3072]{1,0:T(8,128)(2,1)} async-done(((bf16[64,3072]{1,0:T(8,128)(2,1)}), bf16[1024,3072]{1,0:T(8,128)(2,1)}) %all-gather.24.cloned.1.call-update) | async-done | bytes 6291472 | tf_op jit(solution)/shard_map/all_gather | solution.py:268
  417.0 9.1 fusion.153
  426.2 53.6 %all-gather.22.cloned.1.call-done = bf16[1024,3072]{1,0:T(8,128)(2,1)} async-done(((bf16[64,3072]{1,0:T(8,128)(2,1)}), bf16[1024,3072]{1,0:T(8,128)(2,1)}) %all-gather.22.cloned.1.call-update) | async-done | bytes 6291472 | tf_op jit(solution)/shard_map/all_gather | solution.py:267
  479.8 9.2 fusion.152
  489.0 53.5 %all-gather.26.cloned.1.call-done = bf16[3072,1024]{1,0:T(8,128)(2,1)} async-done(((bf16[192,1024]{1,0:T(8,128)(2,1)}), bf16[3072,1024]{1,0:T(8,128)(2,1)}) %all-gather.26.cloned.1.call-update) | async-done | bytes 6291472 | tf_op jit(solution)/shard_map/all_gather | solution.py:269
  542.6 12.1 multiply_convert_fusion
  608.7 11.2 bitcast_dynamic-update-slice_fusion.1
  619.9 11.5 fusion.64
  645.6 88.2 %while.33 = (s32[]{:T(128)}, f32[4096,8,128]{0,2,1:T(8,128)}, f32[4096,8,128]{0,2,1:T(8,128)}, f32[2,128,8,2,128]{4,1,0,3,2:T(8,128)}, f32[2,128,8,128]{3,1,0,2:...) while((s32[]{:T(128)}, f32[4096,8,128]{0,2,1:T(8,128)}, ...), condition=%wide.region_12.13_spmd.clone, body=%wide.region_11.12_spmd.clone.sunk | while | flops 3054141440 | bytes 141462768 | solution.py:402
  677.8 12.1 fusion.234
  721.6 12.2 fusion.234
  733.9 13.9 copy.289
  747.8 9.8 convert_element_type.214
  812.1 8.4 convolution_convert_fusion.1
  829.4 22.0 %reduce-scatter.10.cloned.1.call-done = bf16[256,8,128]{2,0,1:T(8,128)(2,1)} async-done(((bf16[4096,8,128]{2,0,1:T(8,128)(2,1)}), bf16[256,8,128]{2,0,1:T(8,128)(2,1)}) %reduce-scatter.10.cloned.1.call-update) | async-done | bytes 524304 | tf_op jit(solution)/shard_map/reduce_scatter | solution.py:417
  869.6 90.5 %reduce-scatter.12.cloned.1.call-done = bf16[256,8,128]{0,2,1:T(8,128)(2,1)} async-done(((bf16[4096,8,128]{0,2,1:T(8,128)(2,1)}), bf16[256,8,128]{0,2,1:T(8,128)(2,1)}) %reduce-scatter.12.cloned.1.call-update) | async-done | bytes 524304 | tf_op jit(solution)/shard_map/reduce_scatter | solution.py:420
  967.6 9.3 multiply_reduce_fusion.3
  982.2 53.8 %reduce-scatter.20.cloned.1.call-done = bf16[128,1024]{1,0:T(8,128)(2,1)} async-done(((bf16[2048,1024]{1,0:T(8,128)(2,1)}), bf16[128,1024]{1,0:T(8,128)(2,1)}) %reduce-scatter.20.cloned.1.call-update) | async-done | bytes 262160 | tf_op jit(solution)/shard_map/reduce_scatter | solution.py:477
  1036.1 76.0 %reduce-scatter.14.cloned.1.call-done = bf16[64,2048]{1,0:T(8,128)(2,1)} async-done(((bf16[1024,2048]{1,0:T(8,128)(2,1)}), bf16[64,2048]{1,0:T(8,128)(2,1)}) %reduce-scatter.14.cloned.1.call-update) | async-done | bytes 262160 | tf_op jit(solution)/shard_map/reduce_scatter | solution.py:477
  1112.0 88.2 %reduce-scatter.26.cloned.1.call-done = bf16[192,1024]{1,0:T(8,128)(2,1)} async-done(((bf16[3072,1024]{1,0:T(8,128)(2,1)}), bf16[192,1024]{1,0:T(8,128)(2,1)}) %reduce-scatter.26.cloned.1.call-update) | async-done | bytes 393232 | tf_op jit(solution)/shard_map/reduce_scatter | solution.py:313
  1200.2 88.9 %reduce-scatter.24.cloned.1.call-done = bf16[64,3072]{1,0:T(8,128)(2,1)} async-done(((bf16[1024,3072]{1,0:T(8,128)(2,1)}), bf16[64,3072]{1,0:T(8,128)(2,1)}) %reduce-scatter.24.cloned.1.call-update) | async-done | bytes 393232 | tf_op jit(solution)/shard_map/reduce_scatter | solution.py:310
  1289.1 88.3 %reduce-scatter.22.cloned.1.call-done = bf16[64,3072]{1,0:T(8,128)(2,1)} async-done(((bf16[1024,3072]{1,0:T(8,128)(2,1)}), bf16[64,3072]{1,0:T(8,128)(2,1)}) %reduce-scatter.22.cloned.1.call-update) | async-done | bytes 393232 | tf_op jit(solution)/shard_map/reduce_scatter | solution.py:307
  1377.4 65.0 %reduce-scatter.16.cloned.1.call-done = bf16[64,1024]{1,0:T(8,128)(2,1)} async-done(((bf16[1024,1024]{1,0:T(8,128)(2,1)}), bf16[64,1024]{1,0:T(8,128)(2,1)}) %reduce-scatter.16.cloned.1.call-update) | async-done | bytes 131088 | tf_op jit(solution)/shard_map/reduce_scatter | solution.py:477
  1442.4 64.2 %reduce-scatter.18.cloned.1.call-done = bf16[64,1024]{1,0:T(8,128)(2,1)} async-done(((bf16[1024,1024]{1,0:T(8,128)(2,1)}), bf16[64,1024]{1,0:T(8,128)(2,1)}) %reduce-scatter.18.cloned.1.call-update) | async-done | bytes 131088 | tf_op jit(solution)/shard_map/reduce_scatter | solution.py:477
  1520.2 40.5 %psum.95 = f32[4]{0:T(128)S(1)} all-reduce(f32[4]{0:T(128)S(1)} %pad_maximum_fusion.12), channel_id=1, replica_groups=mesh['rep'=2,'fsdp'=16] {'rep','fsdp'}, use_global_device_ids=true, to_apply=%region_50.51 | all-reduce | flops 4 | bytes 32 | tf_op jit(solution)/shard_map/psum | solution.py:499
  1561.3 31.0 %all-reduce.15 = (bf16[1024]{0:T(1024)(128)(2,1)S(1)}, bf16[128]{0:T(256)(128)(2,1)S(1)}, bf16[128]{0:T(256)(128)(2,1)S(1)}, bf16[1024]{0:T(1024)(128)(2,1)S(1)}) all-reduce(bf16[1024]{0:T(1024)(128)(2,1)S(1)} %get-tuple-element.390, bf16[128]{0:T(256)(128)(2,1)S(1)} %get-tuple-element.384, ...), channel_id=4, replica_groups=mesh['rep'=2,'fsdp'=16] {'fsdp'}, use_global_device_ids=true, to_apply=%region_19.20.clone | all-reduce | flops 2304 | bytes 9216
  (464 shorter events, 360.2 us)
Async XLA Ops:
  7.2 47.3 %all-gather.10.cloned.1.call-start = ((), (), s32[]{:S(2)}) async-start(), calls=%async_computation.9 | async-start | bytes 2228224 | tf_op jit(solution)/shard_map/all_gather | solution.py:173
  7.9 88.8 %all-gather.14.cloned.1.call-start = ((), (), s32[]{:S(2)}) async-start(), calls=%async_computation.11 | async-start | bytes 2228224 | tf_op jit(solution)/shard_map/all_gather | solution.py:172
  8.7 139.8 %all-gather.18.cloned.1.call-start = ((), (), s32[]{:S(2)}) async-start(), calls=%async_computation.13 | async-start | bytes 4456448 | tf_op jit(solution)/shard_map/all_gather | solution.py:171
  9.4 218.2 %all-gather.12.cloned.1.call-start = ((), (), s32[]{:S(2)}) async-start(), calls=%async_computation.10 | async-start | bytes 8912896 | tf_op jit(solution)/shard_map/all_gather | solution.py:204
  51.3 97.1 %copy-start.63 = (f32[1024]{0:T(1024)}, f32[1024]{0:T(1024)S(1)}, u32[]{:S(2)}) copy-start(f32[1024]{0:T(1024)S(1)} %convert_element_type.190) | copy-start | bytes 12292
  53.4 95.0 %copy-start.67 = (f32[512]{0:T(512)}, f32[512]{0:T(512)S(1)}, u32[]{:S(2)}) copy-start(f32[512]{0:T(512)S(1)} %fusion.119) | copy-start | bytes 6148
  59.6 243.8 %all-gather.16.cloned.1.call-start = ((), (), s32[]{:S(2)}) async-start(), calls=%async_computation.12 | async-start | bytes 8912896 | tf_op jit(solution)/shard_map/all_gather | solution.py:203
  60.7 99.6 %copy-start.21 = (f32[512,64]{1,0:T(8,128)}, f32[512,64]{1,0:T(8,128)S(1)}, u32[]{:S(2)}) copy-start(f32[512,64]{1,0:T(8,128)S(1)} %get-tuple-element.502) | copy-start | bytes 393220
  60.7 99.6 %copy-start.23 = (f32[512,64]{1,0:T(8,128)}, f32[512,64]{1,0:T(8,128)S(1)}, u32[]{:S(2)}) copy-start(f32[512,64]{1,0:T(8,128)S(1)} %get-tuple-element.503) | copy-start | bytes 393220
  102.6 45.8 %copy-start.26 = (bf16[256,1024]{1,0:T(8,128)(2,1)S(1)}, bf16[256,1024]{1,0:T(8,128)(2,1)}, u32[]{:S(2)}) copy-start(bf16[256,1024]{1,0:T(8,128)(2,1)} %param.22) | copy-start | bytes 1572868
  104.2 251.3 %all-gather.20.cloned.1.call-start = ((), (), s32[]{:S(2)}) async-start(), calls=%async_computation.14 | async-start | bytes 4456448 | tf_op jit(solution)/shard_map/all_gather | solution.py:176
  104.8 312.2 %all-gather.24.cloned.1.call-start = ((), (), s32[]{:S(2)}) async-start(), calls=%async_computation.16 | async-start | bytes 6684672 | tf_op jit(solution)/shard_map/all_gather | solution.py:268
  105.6 374.2 %all-gather.22.cloned.1.call-start = ((), (), s32[]{:S(2)}) async-start(), calls=%async_computation.15 | async-start | bytes 6684672 | tf_op jit(solution)/shard_map/all_gather | solution.py:267
  106.3 436.3 %all-gather.26.cloned.1.call-start = ((), (), s32[]{:S(2)}) async-start(), calls=%async_computation.17 | async-start | bytes 6684672 | tf_op jit(solution)/shard_map/all_gather | solution.py:269
  107.0 744.3 %reduce-scatter.10.cloned.1.call-start = ((), (), s32[]{:S(2)}) async-start(), calls=%async_computation.18 | async-start | bytes 8912896 | tf_op jit(solution)/shard_map/reduce_scatter | solution.py:417
  107.7 457.0 %copy-start.65 = (f32[512]{0:T(512)}, f32[512]{0:T(512)S(1)}, u32[]{:S(2)}) copy-start(f32[512]{0:T(512)S(1)} %pad_convert_fusion) | copy-start | bytes 6148
  107.7 48.7 %copy-start.69 = (f32[128]{0:T(128)}, f32[128]{0:T(128)S(1)}, u32[]{:S(2)}) copy-start(f32[128]{0:T(128)S(1)} %convert_element_type.195) | copy-start | bytes 1540
  360.8 203.9 %copy-start.61 = (f32[512]{0:T(512)}, f32[512]{0:T(512)S(1)}, u32[]{:S(2)}) copy-start(f32[512]{0:T(512)S(1)} %get-tuple-element.510) | copy-start | bytes 6148
  426.2 116.4 %copy-start.40 = (bf16[256,1024]{1,0:T(8,128)(2,1)S(1)}, bf16[256,1024]{1,0:T(8,128)(2,1)}, u32[]{:S(2)}) copy-start(bf16[256,1024]{1,0:T(8,128)(2,1)} %param.37) | copy-start | bytes 1572868
  747.8 212.3 %reduce-scatter.12.cloned.1.call-start = ((), (), s32[]{:S(2)}) async-start(), calls=%async_computation.19 | async-start | bytes 8912896 | tf_op jit(solution)/shard_map/reduce_scatter | solution.py:420
  757.7 278.4 %reduce-scatter.20.cloned.1.call-start = ((), (), s32[]{:S(2)}) async-start(), calls=%async_computation.23 | async-start | bytes 4456448 | tf_op jit(solution)/shard_map/reduce_scatter | solution.py:477
  765.6 346.4 %reduce-scatter.14.cloned.1.call-start = ((), (), s32[]{:S(2)}) async-start(), calls=%async_computation.20 | async-start | bytes 4456448 | tf_op jit(solution)/shard_map/reduce_scatter | solution.py:477
  802.8 397.4 %reduce-scatter.26.cloned.1.call-start = ((), (), s32[]{:S(2)}) async-start(), calls=%async_computation.26 | async-start | bytes 6684672 | tf_op jit(solution)/shard_map/reduce_scatter | solution.py:313
  812.1 477.1 %reduce-scatter.24.cloned.1.call-start = ((), (), s32[]{:S(2)}) async-start(), calls=%async_computation.25 | async-start | bytes 6684672 | tf_op jit(solution)/shard_map/reduce_scatter | solution.py:310
  820.5 556.9 %reduce-scatter.22.cloned.1.call-start = ((), (), s32[]{:S(2)}) async-start(), calls=%async_computation.24 | async-start | bytes 6684672 | tf_op jit(solution)/shard_map/reduce_scatter | solution.py:307
  828.9 613.5 %reduce-scatter.16.cloned.1.call-start = ((), (), s32[]{:S(2)}) async-start(), calls=%async_computation.21 | async-start | bytes 2228224 | tf_op jit(solution)/shard_map/reduce_scatter | solution.py:477
  865.3 96.8 %copy-start.29 = (bf16[256,1024]{1,0:T(8,128)(2,1)S(1)}, bf16[256,1024]{1,0:T(8,128)(2,1)}, u32[]{:S(2)}) copy-start(bf16[256,1024]{1,0:T(8,128)(2,1)} %param.22) | copy-start | bytes 1572868
  865.3 96.8 %copy-start.31 = (bf16[256,1024]{1,0:T(8,128)(2,1)S(1)}, bf16[256,1024]{1,0:T(8,128)(2,1)}, u32[]{:S(2)}) copy-start(bf16[256,1024]{1,0:T(8,128)(2,1)} %param.21) | copy-start | bytes 1572868
  865.3 641.3 %reduce-scatter.18.cloned.1.call-start = ((), (), s32[]{:S(2)}) async-start(), calls=%async_computation.22 | async-start | bytes 2228224 | tf_op jit(solution)/shard_map/reduce_scatter | solution.py:477
  966.1 636.2 %all-reduce.21.cloned.1.call-start = ((), (), s32[]{:S(2)}) async-start(), calls=%async_computation.27 | async-start | bytes 3932160 | tf_op jit(solution)/shard_map/psum | solution.py:497
  1513.7 47.6 %copy-start.75 = (bf16[1024]{0:T(1024)(128)(2,1)S(1)}, bf16[1024]{0:T(1024)(128)(2,1)}, u32[]{:S(2)}) copy-start(bf16[1024]{0:T(1024)(128)(2,1)} %get-tuple-element.388) | copy-start | bytes 6148
  1515.9 84.9 %copy-start.16 = (f32[512,1024]{1,0:T(8,128)S(1)}, f32[512,1024]{1,0:T(8,128)}, u32[]{:S(2)}) copy-start(f32[512,1024]{1,0:T(8,128)} %get-tuple-element.470) | copy-start | bytes 6291460
  (95 other events, 588.1 us)
Sparse Core Ops, SparseCore 0:
  10.2 44.2 all-gather.9
  56.6 40.0 all-gather.13
  98.9 49.4 all-gather.17
  151.0 76.5 all-gather.11
  230.2 73.0 all-gather.15
  305.4 48.9 all-gather.19
  356.7 60.3 all-gather.23
  419.3 60.4 all-gather.21
  482.1 60.4 all-gather.25
  747.9 103.4 reduce-scatter.9
  855.5 104.5 reduce-scatter.11
  963.8 72.2 reduce-scatter.19
  1040.4 71.5 reduce-scatter.13
  1115.8 84.3 reduce-scatter.25
  1204.5 84.5 reduce-scatter.23
  1292.9 84.4 reduce-scatter.21
  1381.5 60.9 reduce-scatter.15
  1446.0 60.5 reduce-scatter.17
  1509.5 61.3 all-reduce.20
where the time goes:
time: 1630 us; the launch traced here: 1620 us
  waiting for transfers between devices  1020 us (63%)
  matrix products  210 us (13%)
  local copies, waits for them, and re-layouts  142 us (9%)
  other arithmetic  114 us (7%)
  blocking collectives  112 us (7%)
  between operations  18.5 us (1%)
    reduce_scatter x4, waiting for transfers between devices, per_device(): lax.psum_scatter(as_sent((grad_first_gain, grad_query, grad_key, grad_val...  259 us
    reduce_scatter x1, waiting for transfers between devices, per_device(): lax.psum_scatter(value_buffer.astype(jnp.bfloat16), 'fsdp', scatter_dimen...  90.5 us
    reduce_scatter x1, waiting for transfers between devices, per_device(): lax.psum_scatter(grad_up.astype(jnp.bfloat16), 'fsdp', scatter_dimension=...  88.9 us
    reduce_scatter x1, waiting for transfers between devices, per_device(): lax.psum_scatter(grad_gate.astype(jnp.bfloat16), 'fsdp', scatter_dimensio...  88.3 us
    reduce_scatter x1, waiting for transfers between devices, per_device(): lax.psum_scatter(grad_down.astype(jnp.bfloat16), 'fsdp', scatter_dimensio...  88.2 us
    all_gather x1, waiting for transfers between devices, per_device(): lax.all_gather(key_reduced[:prompt_on_device], 'fsdp', axis=0, tiled=True)  75.7 us
    unnamed x2, blocking collectives  66.8 us
    all_gather x1, waiting for transfers between devices, per_device(): lax.all_gather(value_matrix_rows[:prompt_on_device], 'fsdp', axis=0, tile...  63.7 us
  transfers between devices with their start and end apart: 19, of which 17 were waited for; matrix products, arithmetic and copies ran while one was open for 15% of the time, Pallas kernels for 0%

commit v1 on v0

--- a/solution.py
+++ b/solution.py
@@ -3,6 +3,8 @@
 import jax
 import jax.numpy as jnp
 from jax import lax
+from jax.experimental import pallas as pl
+from jax.experimental.pallas import tpu as pltpu
 from jax.sharding import PartitionSpec as P
 
 MODEL_WIDTH = 1024
@@ -17,6 +19,231 @@
 norm_epsilon = 1e-06
 rope_theta = 1000000.0
 masked_score = -1e30
+
+
+MESH = pl.DeviceIdType.MESH
+
+def position(n):
+    rep = lax.axis_index("rep")
+    rank = lax.axis_index("fsdp")
+    return rep, rank // 4, (rank // 2) % 2, rank % 2
+
+def gather_kernel(n, m, *refs):
+    A = n // 4
+    own, tile = refs[:m], refs[m]
+    full, tiles = refs[m + 1:2 * m + 1], refs[2 * m + 1]
+    zs, zr, s2s, s2r, s3s, s3r, cs, cr, ls, ts, tr = refs[2 * m + 2:]
+    rep, a, b, c = position(n)
+    h = rep % 2
+    mate = rep + 1 - 2 * h
+    def dev(r, a, b, c):
+        return (r, (a * 2 + b) * 2 + c)
+    barrier = pltpu.get_barrier_semaphore()
+    me = (a * 2 + b) * 2 + c
+    peers = [(rep, (me + d) % n) for d in range(1, n)] + [dev(mate, a, b, c)]
+    for p in peers:
+        pl.semaphore_signal(barrier, inc=1, device_id=p, device_id_type=MESH)
+    pl.semaphore_wait(barrier, len(peers))
+
+    def local(i):
+        return pltpu.make_async_copy(own[i].at[:, h], full[i].at[a, b, c, :, h], ls.at[i])
+    def zc(i, d):
+        return pltpu.make_async_remote_copy(own[i].at[:, h], full[i].at[a, b, c, :, h], zs.at[i, d - 1], zr.at[i, d - 1],
+            device_id=dev(rep, (a + d) % A, b, c), device_id_type=MESH)
+    def pair(ref, ss, rs, to):
+        return pltpu.make_async_remote_copy(ref, ref, ss, rs, device_id=to, device_id_type=MESH)
+    ydev, xdev, cdev = dev(rep, a, 1 - b, c), dev(mate, a, b, c), dev(rep, a, b, 1 - c)
+    def s2(i):
+        return [pair(full[i].at[:, b, c, 0, h], s2s.at[i, 0], s2r.at[i, 0], ydev),
+                pair(full[i].at[:, b, c, 1, h], s2s.at[i, 1], s2r.at[i, 1], xdev)]
+    def s3(i):
+        return [pair(full[i].at[:, :, c, 0, h], s3s.at[i, 0], s3r.at[i, 0], xdev),
+                pair(full[i].at[:, b, c, 1], s3s.at[i, 1], s3r.at[i, 1], ydev)]
+    def s4(i):
+        return [pair(full[i].at[:, :, c], cs.at[i], cr.at[i], cdev)]
+    def share(d):
+        return pltpu.make_async_remote_copy(tile, tiles.at[me], ts.at[d - 1], tr.at[d - 1], device_id=(rep, (me + d) % n), device_id_type=MESH)
+    for d in range(1, n):
+        share(d).start()
+    tiles[me] = tile[...]
+    for i in range(m):
+        local(i).start()
+        for d in range(1, A):
+            zc(i, d).start()
+    for t in range(m + 3):
+        if t < m:
+            local(t).wait()
+            for d in range(1, A):
+                zc(t, d).wait_recv()
+            for q in s2(t): q.start()
+        if 0 <= t - 1 < m:
+            for q in s2(t - 1): q.wait_recv()
+            for q in s3(t - 1): q.start()
+        if 0 <= t - 2 < m:
+            for q in s3(t - 2): q.wait_recv()
+            for q in s4(t - 2): q.start()
+        if 0 <= t - 3 < m:
+            for q in s4(t - 3): q.wait_recv()
+    for d in range(1, n):
+        share(d).wait()
+    for t in range(m):
+        for d in range(1, A):
+            zc(t, d).wait_send()
+        for q in s2(t) + s3(t) + s4(t):
+            q.wait_send()
+
+def gather(shards, tile, n, cid):
+    m = len(shards)
+    A = n // 4
+    views = [s.reshape(2, 2, s.shape[0] // 4, s.shape[1]) for s in shards]
+    outs = [jax.ShapeDtypeStruct((A, 2, 2) + v.shape, v.dtype) for v in views] + [jax.ShapeDtypeStruct((n,) + tile.shape, tile.dtype)]
+    full = pl.pallas_call(
+        partial(gather_kernel, n, m),
+        out_shape=outs,
+        in_specs=[pl.BlockSpec(memory_space=pltpu.VMEM)] * (m + 1),
+        out_specs=[pl.BlockSpec(memory_space=pl.ANY)] * m + [pl.BlockSpec(memory_space=pltpu.VMEM)],
+        scratch_shapes=[pltpu.SemaphoreType.DMA((m, A - 1))] * 2 + [pltpu.SemaphoreType.DMA((m, 2))] * 4 + [pltpu.SemaphoreType.DMA((m,))] * 3 + [pltpu.SemaphoreType.DMA((n - 1,))] * 2,
+        compiler_params=pltpu.CompilerParams(collective_id=cid, has_side_effects=True),
+        name="gather",
+    )(*views, tile)
+    return [f.reshape(-1, s.shape[1]) for f, s in zip(full, shards)], full[m]
+
+
+def add_rows(count, out, first, second, step=None):
+    def one(j, _):
+        o = out(j)
+        total = first(j)[...].astype(jnp.float32)
+        for s in second:
+            total = total + s(j)[...].astype(jnp.float32)
+        o[...] = total.astype(o.dtype)
+        return 0
+    lax.fori_loop(0, count, one, 0)
+
+def scatter_kernel(n, R, m, has_vec, *refs):
+    A = n // 4
+    bits = R.bit_length() - 1
+    it = iter(refs)
+    take = lambda k: [next(it) for _ in range(k)]
+    grads = take(m)
+    vec = next(it) if has_vec else None
+    outs = take(m)
+    vout = next(it) if has_vec else None
+    own, b1, b2y, b2x, b3, b4, b5 = [take(m) for _ in range(7)]
+    s4 = take(m)
+    vb = next(it) if has_vec else None
+    vz = next(it) if has_vec else None
+    ls, s1s, s1r, s2s, s2r, s3s, s3r, s4s, s4r, s5s, s5r, ws = take(12)
+    if has_vec:
+        vs, vr = take(2)
+    rep, a, b, c = position(n)
+    h = rep % 2
+    mate = rep + 1 - 2 * h
+    def dev(r, a, b, c):
+        return (r, (a * 2 + b) * 2 + c)
+    ydev, xdev, cdev = dev(rep, a, 1 - b, c), dev(mate, a, b, c), dev(rep, a, b, 1 - c)
+    zdev = lambda d: dev(rep, (a + d) % A, b, c)
+    def flip(bit):
+        w = 1 << bit
+        return dev(rep + w - 2 * w * ((rep // w) % 2), a, b, c)
+    barrier = pltpu.get_barrier_semaphore()
+    peers = [zdev(d) for d in range(1, A)] + [ydev, xdev, cdev] + [flip(k) for k in range(1, bits)]
+    for p in peers:
+        pl.semaphore_signal(barrier, inc=1, device_id=p, device_id_type=MESH)
+    pl.semaphore_wait(barrier, len(peers))
+    def rc(src, dst, ss, rs, to):
+        return pltpu.make_async_remote_copy(src, dst, ss, rs, device_id=to, device_id_type=MESH)
+    def load(i): return pltpu.make_async_copy(grads[i].at[:, :, c], own[i], ls.at[i])
+    def S1(i): return [rc(grads[i].at[:, :, 1 - c], b1[i], s1s.at[i], s1r.at[i], cdev)]
+    def S2(i): return [rc(b1[i].at[:, 1 - b, 0], b2y[i], s2s.at[i, 0], s2r.at[i, 0], ydev),
+                       rc(b1[i].at[:, :, 1, 1 - h], b2x[i], s2s.at[i, 1], s2r.at[i, 1], xdev)]
+    def S3(i): return [rc(b2y[i].at[:, 1 - h], b3[i].at[0], s3s.at[i, 0], s3r.at[i, 0], xdev),
+                       rc(b2x[i].at[:, 1 - b], b3[i].at[1], s3s.at[i, 1], s3r.at[i, 1], ydev)]
+    def S4(i): return [rc(b3[i].at[:, (a + d) % A], b4[i].at[d - 1], s4s.at[i, d - 1], s4r.at[i, d - 1], zdev(d)) for d in range(1, A)]
+    def S5(i, k): return rc(s4[i].at[0] if k == bits - 1 else s4[i].at[k], b5[i].at[k], s5s.at[i, k], s5r.at[i, k], xdev if k == bits - 1 else flip(k + 1))
+    def put(i, k): return pltpu.make_async_copy((s4[i].at[0] if bits == 1 else s4[i].at[bits - 1]) if k == 0 else b5[i].at[bits - 1], outs[i].at[:, h if k == 0 else 1 - h], ws.at[i, k])
+    for i in range(m):
+        load(i).start()
+        for q in S1(i): q.start()
+    if has_vec:
+        rounds = [cdev, ydev, xdev] + [flip(k) for k in range(1, bits)]
+        vb[0] = vec[...]
+        for k, to in enumerate(rounds):
+            q = rc(vb.at[2 * k], vb.at[2 * k + 1], vs.at[k], vr.at[k], to)
+            q.start(); q.wait()
+            vb[2 * k + 2] = vb[2 * k] + vb[2 * k + 1]
+        last = 2 * len(rounds)
+        nr = len(rounds)
+        qs = [rc(vb.at[last], vz.at[a], vs.at[nr + d - 1], vr.at[nr + d - 1], zdev(d)) for d in range(1, A)]
+        for q in qs: q.start()
+        vz[a] = vb[last]
+        for q in qs: q.wait()
+        total = vz[0]
+        for k in range(1, A):
+            total = total + vz[k]
+        vout[...] = total
+    for t in range(m + 4):
+        i = t
+        if t < m:
+            load(i).wait()
+            for q in S1(i): q.wait_recv()
+            add_rows(A * 2 * 4, lambda j, i=i: b1[i].at[j // 8, (j // 4) % 2, (j // 2) % 2, j % 2],
+                     lambda j, i=i: b1[i].at[j // 8, (j // 4) % 2, (j // 2) % 2, j % 2],
+                     [lambda j, i=i: own[i].at[j // 8, (j // 4) % 2, (j // 2) % 2, j % 2]])
+            for q in S2(i): q.start()
+        i = t - 1
+        if 0 <= i < m:
+            for q in S2(i): q.wait_recv()
+            add_rows(A * 2, lambda j, i=i: b2y[i].at[j // 2, j % 2], lambda j, i=i: b2y[i].at[j // 2, j % 2],
+                     [lambda j, i=i: b1[i].at[j // 2, b, 0, j % 2]])
+            add_rows(A * 2, lambda j, i=i: b2x[i].at[j // 2, j % 2], lambda j, i=i: b2x[i].at[j // 2, j % 2],
+                     [lambda j, i=i: b1[i].at[j // 2, j % 2, 1, h]])
+            for q in S3(i): q.start()
+        i = t - 2
+        if 0 <= i < m:
+            for q in S3(i): q.wait_recv()
+            add_rows(A, lambda j, i=i: b3[i].at[0, j], lambda j, i=i: b3[i].at[0, j], [lambda j, i=i: b2y[i].at[j, h]])
+            add_rows(A, lambda j, i=i: b3[i].at[1, j], lambda j, i=i: b3[i].at[1, j], [lambda j, i=i: b2x[i].at[j, b]])
+            for q in S4(i): q.start()
+        i = t - 3
+        if 0 <= i < m:
+            for q in S4(i): q.wait_recv()
+            add_rows(2, lambda j, i=i: s4[i].at[0, j], lambda j, i=i: b3[i].at[j, a], [lambda j, i=i, d=d: b4[i].at[d, j] for d in range(A - 1)])
+            for k in range(bits - 1):
+                q = S5(i, k); q.start(); q.wait()
+                add_rows(2, lambda j, i=i, k=k: s4[i].at[k + 1, j], lambda j, i=i, k=k: s4[i].at[k, j], [lambda j, i=i, k=k: b5[i].at[k, j]])
+            rc(s4[i].at[bits - 1], b5[i].at[bits - 1], s5s.at[i, bits - 1], s5r.at[i, bits - 1], xdev).start()
+            put(i, 0).start()
+        i = t - 4
+        if 0 <= i < m:
+            rc(s4[i].at[bits - 1], b5[i].at[bits - 1], s5s.at[i, bits - 1], s5r.at[i, bits - 1], xdev).wait_recv()
+            put(i, 1).start()
+    for i in range(m):
+        for q in S1(i) + S2(i) + S3(i) + S4(i): q.wait_send()
+        rc(s4[i].at[bits - 1], b5[i].at[bits - 1], s5s.at[i, bits - 1], s5r.at[i, bits - 1], xdev).wait_send()
+        put(i, 0).wait(); put(i, 1).wait()
+
+def scatter(grads, n, R, cid, vec=None):
+    m, A, bits = len(grads), n // 4, R.bit_length() - 1
+    views = [g.reshape(A, 2, 2, 2, 2, g.shape[0] // (4 * n), g.shape[1]) for g in grads]
+    sub = [v.shape[-2:] for v in views]
+    bf = jnp.bfloat16
+    V, D = pltpu.VMEM, pltpu.SemaphoreType.DMA
+    scratch = ([V((A, 2, 2, 2) + s, bf) for s in sub] * 2 + [V((A, 2) + s, bf) for s in sub] * 2 + [V((2, A) + s, bf) for s in sub]
+        + [V((A - 1, 2) + s, bf) for s in sub] + [V((bits, 2) + s, bf) for s in sub] + [V((bits, 2) + s, bf) for s in sub])
+    ins, ispec = list(views), [pl.BlockSpec(memory_space=pl.ANY)] * m
+    outs, ospec = [jax.ShapeDtypeStruct((2, 2) + s, bf) for s in sub], [pl.BlockSpec(memory_space=pl.ANY)] * m
+    sems = [D((m,)), D((m,)), D((m,)), D((m, 2)), D((m, 2)), D((m, 2)), D((m, 2)), D((m, A - 1)), D((m, A - 1)), D((m, bits)), D((m, bits)), D((m, 2))]
+    if vec is not None:
+        ins.append(vec); ispec.append(pl.BlockSpec(memory_space=pltpu.VMEM))
+        outs.append(jax.ShapeDtypeStruct(vec.shape, vec.dtype)); ospec.append(pl.BlockSpec(memory_space=pltpu.VMEM))
+        scratch += [V((2 * (2 + bits) + 1,) + vec.shape, vec.dtype), V((A,) + vec.shape, vec.dtype)]
+        sems += [D((2 + bits + A - 1,))] * 2
+    res = pl.pallas_call(partial(scatter_kernel, n, R, m, vec is not None), out_shape=outs, in_specs=ispec, out_specs=ospec,
+        scratch_shapes=scratch + sems,
+        compiler_params=pltpu.CompilerParams(collective_id=cid, has_side_effects=True, vmem_limit_bytes=60 << 20),
+        name="scatter")(*ins)
+    shards = [r.reshape(-1, r.shape[-1]) for r in res[:m]]
+    return (shards, res[m]) if vec is not None else shards
 
 
 def as_sent(shard):
@@ -166,18 +393,27 @@
             axis=1,
         )
 
-    attention_set = (
-        lax.all_gather(attention_gain, "fsdp", axis=0, tiled=True),
-        lax.all_gather(query_weight, "fsdp", axis=0, tiled=True),
-        lax.all_gather(key_matrix, "fsdp", axis=0, tiled=True),
-        lax.all_gather(value_matrix, "fsdp", axis=0, tiled=True),
-        lax.all_gather(query_gain, "fsdp", axis=0, tiled=True),
-        lax.all_gather(key_norm_gain, "fsdp", axis=0, tiled=True),
-        lax.all_gather(out_weight, "fsdp", axis=0, tiled=True),
-    )
-    gain_first, query_full, key_full, value_full, query_scale, key_norm_scale, out_full = (
-        attention_set
-    )
+    n = lax.axis_size("fsdp")
+    R = lax.axis_size("rep")
+    tile = jnp.stack(
+        [
+            jnp.pad(v.astype(jnp.float32), (0, 128 - v.shape[0]))
+            for v in (attention_gain, mlp_gain, query_gain, key_norm_gain)
+        ]
+    )
+    tile = jnp.pad(tile, ((0, 4), (0, 0)))
+    (key_full, value_full, query_full, out_full, gate_full, up_full, down_full), tiles = gather(
+        [key_matrix, value_matrix, query_weight, out_weight, gate_weight, up_weight, down_weight],
+        tile,
+        n,
+        0,
+    )
+    gain_first = tiles[:, 0, : attention_gain.shape[0]].reshape(-1)
+    gain_second = tiles[:, 1, : mlp_gain.shape[0]].reshape(-1)
+    query_scale = tiles[:, 2, : query_gain.shape[0]].reshape(-1)
+    key_norm_scale = tiles[:, 3, : key_norm_gain.shape[0]].reshape(-1)
+    query_back, key_back, value_back, out_back = query_full, key_full, value_full, out_full
+    gate_back, up_back, down_back = gate_full, up_full, down_full
     rows_wide = jnp.concatenate([prompt_rows, suffix_rows], 0).astype(jnp.float32)
     hidden_wide, first_pull = jax.vjp(root_mean_scale, rows_wide, gain_first.astype(jnp.float32))
     hidden_state = hidden_wide.astype(jnp.bfloat16)
@@ -262,13 +498,6 @@
     attended = attended_group.reshape(number_of_rows, QUERY_HEADS * HEAD_SIZE)
     attended_low = attended.astype(jnp.bfloat16)
     residual = rows_wide + jnp.dot(attended_low, out_full, preferred_element_type=jnp.float32)
-    mlp_set = (
-        lax.all_gather(mlp_gain, "fsdp", axis=0, tiled=True),
-        lax.all_gather(gate_weight, "fsdp", axis=0, tiled=True),
-        lax.all_gather(up_weight, "fsdp", axis=0, tiled=True),
-        lax.all_gather(down_weight, "fsdp", axis=0, tiled=True),
-    )
-    gain_second, gate_full, up_full, down_full = mlp_set
     hidden_two_wide, second_pull = jax.vjp(
         root_mean_scale, residual, gain_second.astype(jnp.float32)
     )
@@ -278,11 +507,6 @@
     act_wide, act_pull = jax.vjp(swiglu, gate_pre, up_pre)
     act_low = act_wide.astype(jnp.bfloat16)
     mixed_full = residual + jnp.dot(act_low, down_full, preferred_element_type=jnp.float32)
-    gate_back, up_back, down_back = (
-        lax.all_gather(gate_weight, "fsdp", axis=0, tiled=True),
-        lax.all_gather(up_weight, "fsdp", axis=0, tiled=True),
-        lax.all_gather(down_weight, "fsdp", axis=0, tiled=True),
-    )
     d_mixed = (
         jnp.concatenate([prompt_cotangent, suffix_cotangent], 0).astype(jnp.float32)
         * valid_rows[:, None]
@@ -300,26 +524,6 @@
     ) + jnp.einsum("rf,df->rd", d_up, up_back, preferred_element_type=jnp.float32)
     d_resid_mlp, grad_second_gain = second_pull(d_hidden_two)
     d_resid = d_mixed + d_resid_mlp
-    mlp_shards = (
-        lax.psum_scatter(
-            grad_second_gain.astype(jnp.bfloat16), "fsdp", scatter_dimension=0, tiled=True
-        ).astype(jnp.float32),
-        lax.psum_scatter(
-            grad_gate.astype(jnp.bfloat16), "fsdp", scatter_dimension=0, tiled=True
-        ).astype(jnp.float32),
-        lax.psum_scatter(
-            grad_up.astype(jnp.bfloat16), "fsdp", scatter_dimension=0, tiled=True
-        ).astype(jnp.float32),
-        lax.psum_scatter(
-            grad_down.astype(jnp.bfloat16), "fsdp", scatter_dimension=0, tiled=True
-        ).astype(jnp.float32),
-    )
-    query_back, key_back, value_back, out_back = (
-        lax.all_gather(query_weight, "fsdp", axis=0, tiled=True),
-        lax.all_gather(key_matrix, "fsdp", axis=0, tiled=True),
-        lax.all_gather(value_matrix, "fsdp", axis=0, tiled=True),
-        lax.all_gather(out_weight, "fsdp", axis=0, tiled=True),
-    )
     d_resid_low = d_resid.astype(jnp.bfloat16)
     grad_out = jnp.einsum(
         "ra,rd->ad", attended_low, d_resid_low, preferred_element_type=jnp.float32
@@ -471,51 +675,54 @@
             jnp.sum(valid_rows),
         ]
     )
-    stat_extra = ()
-    attention_shards = jax.tree.map(
-        lambda part: part.astype(jnp.float32),
-        lax.psum_scatter(
-            as_sent(
-                (
-                    grad_first_gain,
-                    grad_query,
-                    grad_key,
-                    grad_value,
-                    grad_query_scale,
-                    grad_key_scale,
-                    grad_out,
-                )
-                + stat_extra
-            ),
-            "fsdp",
-            scatter_dimension=0,
-            tiled=True,
-        ),
-    )
-    summed = jax.tree.map(
-        lambda part: part.astype(jnp.float32),
-        lax.psum(as_sent(attention_shards + mlp_shards), "rep"),
-    )
-    stat_sums = lax.psum(stats, ("rep", "fsdp"))
+    vec = jnp.concatenate(
+        [grad_first_gain, grad_second_gain, grad_query_scale, grad_key_scale, jnp.pad(stats, (0, 124))]
+    )
+    vec = jnp.pad(vec.reshape(-1, 128), ((0, (-vec.shape[0] // 128) % 8), (0, 0)))
+    bf = jnp.bfloat16
+    shards, vec_sum = scatter(
+        [
+            grad_down.astype(bf),
+            grad_gate.astype(bf),
+            grad_up.astype(bf),
+            grad_out.astype(bf),
+            grad_query.astype(bf),
+            grad_key.astype(bf),
+            grad_value.astype(bf),
+        ],
+        n,
+        R,
+        1,
+        vec,
+    )
+    g_down, g_gate, g_up, g_out, g_query, g_key, g_value = [g.astype(jnp.float32) for g in shards]
+    flat = vec_sum.reshape(-1)
+    def mine(first, whole, part):
+        return lax.dynamic_slice_in_dim(flat[first : first + whole], fsdp_rank * part, part)
+    w = MODEL_WIDTH
+    g_first = mine(0, w, attention_gain.shape[0])
+    g_second = mine(w, w, mlp_gain.shape[0])
+    g_qs = mine(2 * w, HEAD_SIZE, query_gain.shape[0])
+    g_ks = mine(2 * w + HEAD_SIZE, HEAD_SIZE, key_norm_gain.shape[0])
+    stat_sums = flat[2 * w + 2 * HEAD_SIZE : 2 * w + 2 * HEAD_SIZE + 4]
     token_norms = jnp.sqrt(stat_sums[:3] / (stat_sums[3] * MODEL_WIDTH))
     mixed_low = mixed_full.astype(jnp.bfloat16)
-    mlp_done = summed[-4:]
     return (
         mixed_low[:prompt_on_device],
         mixed_low[prompt_on_device:],
         d_rows[:prompt_on_device],
         d_rows[prompt_on_device:],
-        summed[0],
-        summed[1],
-        summed[2],
-        summed[3],
-        summed[4],
-        summed[5],
-        summed[6],
-        mlp_done[0],
-        mlp_done[1],
-        mlp_done[2],
-        mlp_done[3],
+        g_first,
+        g_query,
+        g_key,
+        g_value,
+        g_qs,
+        g_ks,
+        g_out,
+        g_second,
+        g_gate,
+        g_up,
+        g_down,
         token_norms,
     )
 

time: 1630 us -> 1150 us (0.71)
  waiting for transfers between devices: 1020 us -> 272 us
  Pallas kernels: 0 us -> 342 us
  blocking collectives: 112 us -> 0 us
  local copies, waits for them, and re-layouts: 142 us -> 231 us
  matrix products: 210 us -> 176 us
  other arithmetic: 114 us -> 95.2 us
    reduce_scatter x7 -> x0, waiting for transfers between devices: 524 us -> none  [the longest x4 259 us: per_device(): lax.psum_scatter(as_sent((grad_first_gain, grad_query, grad_key, grad_val...]
    pallas_call x0 -> x2, Pallas kernels: none -> 342 us  [the longest x1 173 us: gather(): pl.pallas_call(partial(gather_kernel, n, m), out_shape=outs, in_specs=[pl...]
    all_gather x7 -> x0, waiting for transfers between devices: 236 us -> none  [the longest x1 53.6 us: per_device(): lax.all_gather(gate_weight, 'fsdp', axis=0, tiled=True)]
    reduce_scatter x1, waiting for transfers between devices: 22 us -> 99.5 us  [per_device(): lax.psum_scatter(key_buffer.astype(jnp.bfloat16), 'fsdp', scatter_dimensi...]
    unnamed x2 -> x0, blocking collectives: 66.8 us -> none
    dynamic_update_slice x4 -> x2, local copies, waits for them, and re-layouts: 2.97 us -> 53.2 us  [per_device(): lax.map(slot_forward, (slot_query_rows, slot_key_rows, slot_value_rows, o...]
    reduce_scatter x1, waiting for transfers between devices: 90.5 us -> 43 us  [per_device(): lax.psum_scatter(value_buffer.astype(jnp.bfloat16), 'fsdp', scatter_dimen...]
    psum x2 -> x0, blocking collectives: 45.4 us -> none  [the longest x1 40.5 us: per_device(): stat_sums = lax.psum(stats, ('rep', 'fsdp'))]
  transfers between devices with their start and end apart: 19 -> 4, of which waited for: 17 -> 4; matrix products, arithmetic and copies ran while one was open for 15% -> 9% of each run, Pallas kernels for 0% -> 0%
where the time goes in v1:
time: 1150 us; the launch traced here: 1140 us
  Pallas kernels  342 us (30%)
  waiting for transfers between devices  272 us (24%)
  local copies, waits for them, and re-layouts  231 us (20%)
  matrix products  176 us (15%)
  other arithmetic  95.2 us (8%)
  between operations  16 us (1%)
    pallas_call x1, Pallas kernels, gather(): pl.pallas_call(partial(gather_kernel, n, m), out_shape=outs, in_specs=[pl...  173 us
    pallas_call x1, Pallas kernels, scatter(): pl.pallas_call(partial(scatter_kernel, n, R, m, vec is not None), out_sha...  169 us
    reduce_scatter x1, waiting for transfers between devices, per_device(): lax.psum_scatter(key_buffer.astype(jnp.bfloat16), 'fsdp', scatter_dimensi...  99.5 us
    all_gather x1, waiting for transfers between devices, per_device(): lax.all_gather(value_matrix_rows[:prompt_on_device], 'fsdp', axis=0, tile...  67 us
    all_gather x1, waiting for transfers between devices, per_device(): lax.all_gather(key_reduced[:prompt_on_device], 'fsdp', axis=0, tiled=True)  62.4 us
    dynamic_update_slice x2, local copies, waits for them, and re-layouts, per_device(): lax.map(slot_forward, (slot_query_rows, slot_key_rows, slot_value_rows, o...  53.2 us
    reduce_scatter x1, waiting for transfers between devices, per_device(): lax.psum_scatter(value_buffer.astype(jnp.bfloat16), 'fsdp', scatter_dimen...  43 us
    unnamed x181, local copies, waits for them, and re-layouts  42.4 us
  transfers between devices with their start and end apart: 4, of which 4 were waited for; matrix products, arithmetic and copies ran while one was open for 9% of the time, Pallas kernels for 0%

profile of v1, /device:TPU:0, one launch (start us, length us, event | category | flops | bytes accessed | tf_op | source)
XLA Modules:
  0.0 1135.6 jit_solution(4036773928154632561)
XLA Ops:
  9.3 172.6 %gather.1 = (bf16[4,2,2,2,2,16,1024]{6,5,4,3,2,1,0:T(8,128)(2,1)}, bf16[4,2,2,2,2,16,1024]{6,5,4,3,2,1,0:T(8,128)(2,1)}, bf16[4,2,2,2,2,16,2048]{6,5,4,3,2,1,0:T...) custom-call(bf16[2,2,16,1024]{3,2,1,0:T(8,128)(2,1)} %bitcast.479, ...), custom_call_target="tpu_custom_call" | custom-call | tf_op jit(solution)/shard_map/gather/pallas_call | solution.py:100
  199.1 6.4 copy.74
  217.9 62.4 %all-gather.5.cloned.1.call-done = bf16[4096,8,128]{0,2,1:T(8,128)(2,1)} async-done(((bf16[256,8,128]{0,2,1:T(8,128)(2,1)}), bf16[4096,8,128]{0,2,1:T(8,128)(2,1)}) %all-gather.5.cloned.1.call-update) | async-done | bytes 8388624 | tf_op jit(solution)/shard_map/all_gather | solution.py:439
  280.4 12.0 %copy.79 = bf16[4096,8,128]{2,0,1:T(8,128)(2,1)} copy(bf16[4096,8,128]{0,2,1:T(8,128)(2,1)} %all-gather.5.cloned.1.call-done) | data formatting | bytes 16777216
  292.4 67.0 %all-gather.3.cloned.1.call-done = bf16[4096,8,128]{0,2,1:T(8,128)(2,1)} async-done(((bf16[256,8,128]{0,2,1:T(8,128)(2,1)}), bf16[4096,8,128]{0,2,1:T(8,128)(2,1)}) %all-gather.3.cloned.1.call-update) | async-done | bytes 8388624 | tf_op jit(solution)/shard_map/all_gather | solution.py:440
  359.4 24.8 %while.32 = (s32[]{:T(128)}, f32[2,128,8,2,128]{1,4,3,2,0:T(8,128)}, f32[2,8,2,128]{3,2,1,0:T(2,128)S(1)}, s32[2]{0:T(128)S(1)}, bf16[4096,8,128]{0,2,1:T(8,128)...) while((s32[]{:T(128)}, ...), condition=%wide.region_8.9_spmd.clone, body=%wide.region_5.8_spmd.clone.sunk | while | flops 1245739008 | bytes 66224836 | solution.py:486
  405.3 6.4 fusion.161
  414.0 5.5 multiply_reduce_fusion.9
  430.6 11.9 %multiply_convert_fusion = (bf16[512,3072]{1,0:T(8,128)(2,1)}, bf16[512,3072]{1,0:T(8,128)(2,1)}, bf16[512,3072]{1,0:T(8,128)(2,1)}) fusion(f32[512,3072]{1,0:T(8,128)} %fusion.162, f32[512,3072]{1,0:T(8,128)} %fusion.163, bf16[3072,1024]{1,0:T(8,128)(2,1)S(1)} %bitcast.490, f32[512]{0:T(512)S(1)} %pad_convert_fusion, ...), kind=kOutput, calls=%fused_computation.101 | convolution fusion | flops 3249537024 | bytes 29362176 | tf_op jit(solution)/shard_map/rd,fd->rf/dot_general | solution.py:516
  442.4 6.7 fusion.164
  449.1 6.6 multiply_reduce_fusion.6
  479.9 7.4 copy.126
  491.9 7.9 broadcast.281.clone.1
  499.7 11.2 bitcast_dynamic-update-slice_fusion.1
  510.9 11.5 %fusion.63 = bf16[8,2,256,1024]{2,3,1,0:T(8,128)(2,1)} fusion(f32[8,1024,256,2]{2,1,3,0:T(8,128)} %copy-done.3, bf16[256,8,2,128]{0,3,2,1:T(8,128)(2,1)S(1)} %bitcast.464, f32[8,2,256]{2,1,0:T(2,128)S(1)} %get-tuple-element.414, f32[8,2,256]{2,1,0:T(2,128)S(1)} %bitcast.485, pred[256,1024]{0,1:T(8,128)(4,1)S(1)} %iota_compare_fusion.2, ...), kind=kOutput, calls=%fused_computation.88 | convolution fusion | flops 1098907648 | bytes 28606468 | tf_op jit(solution)/shard_map/rhgd,khd->hgrk/dot_general | solution.py:331
  524.5 6.2 bitcast_dynamic-update-slice_fusion.2
  530.8 5.8 copy-done.2
  536.6 163.6 %while.33 = (s32[]{:T(128)}, f32[4096,8,128]{0,2,1:T(8,128)}, f32[4096,8,128]{0,2,1:T(8,128)}, f32[2,128,8,2,128]{1,0,4,3,2:T(2,128)}, f32[2,128,8,128]{1,0,3,2:...) while((s32[]{:T(128)}, f32[4096,8,128]{0,2,1:T(8,128)}, ...), condition=%wide.region_12.13_spmd.clone, body=%wide.region_11.12_spmd.clone.sunk | while | flops 3054141440 | bytes 152997072 | solution.py:606
  564.1 14.0 %dynamic_update_slice.57 = f32[2,128,8,128]{1,0,3,2:T(2,128)} dynamic-update-slice(f32[2,128,8,128]{1,0,3,2:T(2,128)} %get-tuple-element.678, f32[1,128,8,128]{1,0,3,2:T(1,128)S(1)} %bitcast.438, s32[]{:T(128)S(6)} %copy.232, s32[]{:T(128)} %constant.167.clone.1..sunk.1, s32[]{:T(128)} %constant.167.clone.1..sunk.1, s32[]{:T(128)} %constant.167.clone.1..sunk.1) | dynamic-update-slice | bytes 1048580 | tf_op jit(solution)/shard_map/while/body/jit(dynamic_update_index_in_dim)/dynamic_update_slice | solution.py:606
  579.8 26.6 %dynamic_update_slice.56 = f32[2,128,8,2,128]{1,0,4,3,2:T(2,128)} dynamic-update-slice(f32[2,128,8,2,128]{1,0,4,3,2:T(2,128)} %get-tuple-element.677, f32[1,128,8,2,128]{1,0,4,3,2:T(1,128)S(1)} %bitcast.440, s32[]{:T(128)S(6)} %copy.232, s32[]{:T(128)} %constant.167.clone.1..sunk.1, s32[]{:T(128)} %constant.167.clone.1..sunk.1, s32[]{:T(128)} %constant.167.clone.1..sunk.1, s32[]{:T(128)} %constant.167.clone.1..sunk.1) | dynamic-update-slice | bytes 2097156 | tf_op jit(solution)/shard_map/while/body/jit(dynamic_update_index_in_dim)/dynamic_update_slice | solution.py:486
  606.4 12.1 %fusion.238 = (f32[4096,8,128]{0,2,1:T(8,128)}, f32[4096,8,128]{0,2,1:T(8,128)}) fusion(f32[4096,8,128]{0,2,1:T(8,128)} %get-tuple-element.676, s32[]{:T(128)S(6)} %select_n.148, f32[1152,8,128]{0,2,1:T(8,128)} %fusion.235, f32[4096,8,128]{0,2,1:T(8,128)} %get-tuple-element.675, f32[1152,8,128]{0,2,1:T(8,128)} %copy-done), kind=kLoop, calls=%fused_computation.52.clone.1 | loop fusion | flops 2097152 | bytes 25165828 | tf_op jit(solution)/shard_map/while/body/eval_jaxpr/dynamic_update_slice | solution.py:594
  645.6 14.0 %dynamic_update_slice.57 = f32[2,128,8,128]{1,0,3,2:T(2,128)} dynamic-update-slice(f32[2,128,8,128]{1,0,3,2:T(2,128)} %get-tuple-element.678, f32[1,128,8,128]{1,0,3,2:T(1,128)S(1)} %bitcast.438, s32[]{:T(128)S(6)} %copy.232, s32[]{:T(128)} %constant.167.clone.1..sunk.1, s32[]{:T(128)} %constant.167.clone.1..sunk.1, s32[]{:T(128)} %constant.167.clone.1..sunk.1) | dynamic-update-slice | bytes 1048580 | tf_op jit(solution)/shard_map/while/body/jit(dynamic_update_index_in_dim)/dynamic_update_slice | solution.py:606
  661.4 26.6 %dynamic_update_slice.56 = f32[2,128,8,2,128]{1,0,4,3,2:T(2,128)} dynamic-update-slice(f32[2,128,8,2,128]{1,0,4,3,2:T(2,128)} %get-tuple-element.677, f32[1,128,8,2,128]{1,0,4,3,2:T(1,128)S(1)} %bitcast.440, s32[]{:T(128)S(6)} %copy.232, s32[]{:T(128)} %constant.167.clone.1..sunk.1, s32[]{:T(128)} %constant.167.clone.1..sunk.1, s32[]{:T(128)} %constant.167.clone.1..sunk.1, s32[]{:T(128)} %constant.167.clone.1..sunk.1) | dynamic-update-slice | bytes 2097156 | tf_op jit(solution)/shard_map/while/body/jit(dynamic_update_index_in_dim)/dynamic_update_slice | solution.py:486
  688.0 12.1 %fusion.238 = (f32[4096,8,128]{0,2,1:T(8,128)}, f32[4096,8,128]{0,2,1:T(8,128)}) fusion(f32[4096,8,128]{0,2,1:T(8,128)} %get-tuple-element.676, s32[]{:T(128)S(6)} %select_n.148, f32[1152,8,128]{0,2,1:T(8,128)} %fusion.235, f32[4096,8,128]{0,2,1:T(8,128)} %get-tuple-element.675, f32[1152,8,128]{0,2,1:T(8,128)} %copy-done), kind=kLoop, calls=%fused_computation.52.clone.1 | loop fusion | flops 2097152 | bytes 25165828 | tf_op jit(solution)/shard_map/while/body/eval_jaxpr/dynamic_update_slice | solution.py:594
  700.2 9.0 convert_element_type.191
  709.2 10.1 convert_element_type.187
  725.5 6.3 fusion.100
  752.6 5.9 convolution_convert_fusion.2
  758.5 5.5 convolution_convert_fusion
  769.4 43.0 %reduce-scatter.5.cloned.1.call-done = bf16[256,8,128]{0,2,1:T(8,128)(2,1)} async-done(((bf16[4096,8,128]{0,2,1:T(8,128)(2,1)}), bf16[256,8,128]{0,2,1:T(8,128)(2,1)}) %reduce-scatter.5.cloned.1.call-update) | async-done | bytes 524304 | tf_op jit(solution)/shard_map/reduce_scatter | solution.py:624
  821.4 99.5 %reduce-scatter.3.cloned.1.call-done = bf16[256,8,128]{0,2,1:T(8,128)(2,1)} async-done(((bf16[4096,8,128]{0,2,1:T(8,128)(2,1)}), bf16[256,8,128]{0,2,1:T(8,128)(2,1)}) %reduce-scatter.3.cloned.1.call-update) | async-done | bytes 524304 | tf_op jit(solution)/shard_map/reduce_scatter | solution.py:621
  941.2 169.2 %scatter.1 = (bf16[2,2,48,1024]{3,2,1,0:T(8,128)(2,1)}, bf16[2,2,16,3072]{3,2,1,0:T(8,128)(2,1)}, bf16[2,2,16,3072]{3,2,1,0:T(8,128)(2,1)}, bf16[2,2,32,1024]{3,...) custom-call(bf16[4,2,2,2,2,48,1024]{6,5,4,3,2,1,0:T(8,128)(2,1)} %bi, ...), custom_call_target="tpu_custom_call" | custom-call | tf_op jit(solution)/shard_map/scatter/pallas_call | solution.py:241
  (444 shorter events, 254.7 us)
Async XLA Ops:
  7.2 176.7 %copy-start.27 = (bf16[256,1024]{1,0:T(8,128)(2,1)S(1)}, bf16[256,1024]{1,0:T(8,128)(2,1)}, u32[]{:S(2)}) copy-start(bf16[256,1024]{1,0:T(8,128)(2,1)} %param.22) | copy-start | bytes 1572868
  7.2 176.7 %copy-start.31 = (bf16[256,1024]{1,0:T(8,128)(2,1)S(1)}, bf16[256,1024]{1,0:T(8,128)(2,1)}, u32[]{:S(2)}) copy-start(bf16[256,1024]{1,0:T(8,128)(2,1)} %param.21) | copy-start | bytes 1572868
  7.2 273.2 %all-gather.5.cloned.1.call-start = ((), (), s32[]{:S(2)}) async-start(), calls=%async_computation.3 | async-start | bytes 8912896 | tf_op jit(solution)/shard_map/all_gather | solution.py:439
  184.2 21.2 %copy-start.74 = (f32[512]{0:T(512)}, f32[512]{0:T(512)S(1)}, u32[]{:S(2)}) copy-start(f32[512]{0:T(512)S(1)} %fusion.128) | copy-start | bytes 6148
  184.4 21.1 %copy-start.70 = (f32[1024]{0:T(1024)}, f32[1024]{0:T(1024)S(1)}, u32[]{:S(2)}) copy-start(f32[1024]{0:T(1024)S(1)} %mul.514) | copy-start | bytes 12292
  191.9 19.6 %copy-start.23 = (f32[512,64]{0,1:T(8,128)}, f32[512,64]{0,1:T(8,128)S(1)}, u32[]{:S(2)}) copy-start(f32[512,64]{0,1:T(8,128)S(1)} %get-tuple-element.419) | copy-start | bytes 393220
  191.9 19.6 %copy-start.25 = (f32[512,64]{0,1:T(8,128)}, f32[512,64]{0,1:T(8,128)S(1)}, u32[]{:S(2)}) copy-start(f32[512,64]{0,1:T(8,128)S(1)} %get-tuple-element.420) | copy-start | bytes 393220
  193.8 165.6 %all-gather.3.cloned.1.call-start = ((), (), s32[]{:S(2)}) async-start(), calls=%async_computation.2 | async-start | bytes 8912896 | tf_op jit(solution)/shard_map/all_gather | solution.py:440
  197.8 614.5 %reduce-scatter.5.cloned.1.call-start = ((), (), s32[]{:S(2)}) async-start(), calls=%async_computation.5 | async-start | bytes 8912896 | tf_op jit(solution)/shard_map/reduce_scatter | solution.py:624
  198.1 12.1 %copy-start.78 = (f32[128]{0:T(128)}, f32[128]{0:T(128)S(1)}, u32[]{:S(2)}) copy-start(f32[128]{0:T(128)S(1)} %mul.538) | copy-start | bytes 1540
  217.6 74.8 %copy-start.81 = (pred[256]{0:T(512)(128)(4,1)}, pred[256]{0:T(512)(128)(4,1)S(1)}, u32[]{:S(2)}) copy-start(pred[256]{0:T(512)(128)(4,1)S(1)} %bitcast_compare_fusion) | copy-start | bytes 772
  217.6 238.0 %copy-start.72 = (f32[512]{0:T(512)}, f32[512]{0:T(512)S(1)}, u32[]{:S(2)}) copy-start(f32[512]{0:T(512)S(1)} %pad_convert_fusion) | copy-start | bytes 6148
  405.3 8.7 copy-start.28
  413.9 11.2 slice-start.6
  419.4 36.3 %copy-start.68 = (f32[512]{0:T(512)}, f32[512]{0:T(512)S(1)}, u32[]{:S(2)}) copy-start(f32[512]{0:T(512)S(1)} %get-tuple-element.429) | copy-start | bytes 6148
  419.4 36.3 %copy-start.15 = (f32[512,1024]{1,0:T(8,128)}, f32[512,1024]{1,0:T(8,128)S(1)}, u32[]{:S(2)}) copy-start(f32[512,1024]{1,0:T(8,128)S(1)} %get-tuple-element.430) | copy-start | bytes 6291460
  419.8 10.8 slice-start
  606.4 12.1 %copy-start.10 = (bf16[2,128,8,128]{3,1,2,0:T(8,128)(2,1)S(1)}, bf16[2,128,8,128]{3,1,2,0:T(8,128)(2,1)}, u32[]{:S(2)}) copy-start(bf16[2,128,8,128]{3,1,2,0:T(8,128)(2,1)} %copy-done.9) | copy-start | bytes 1572868 | tf_op jit(solution)/shard_map/while
  606.4 12.1 %copy-start.59 = (f32[2,8,2,128]{3,0,1,2:T(2,128)S(1)}, f32[2,8,2,128]{3,0,1,2:T(2,128)}, u32[]{:S(2)}) copy-start(f32[2,8,2,128]{3,0,1,2:T(2,128)} %copy-done.58) | copy-start | bytes 49156 | tf_op jit(solution)/shard_map/while
  606.4 12.1 %copy-start.63 = (f32[2,8,2,128]{3,2,1,0:T(2,128)S(1)}, f32[2,8,2,128]{3,2,1,0:T(2,128)}, u32[]{:S(2)}) copy-start(f32[2,8,2,128]{3,2,1,0:T(2,128)} %copy-done.62) | copy-start | bytes 49156 | tf_op jit(solution)/shard_map/while
  606.4 12.1 %copy-start.88 = (pred[2,128]{1,0:T(4,128)(4,1)S(1)}, pred[2,128]{1,0:T(4,128)(4,1)}, u32[]{:S(2)}) copy-start(pred[2,128]{1,0:T(4,128)(4,1)} %copy-done.87) | copy-start | bytes 772 | tf_op jit(solution)/shard_map/while
  606.4 12.1 %copy-start.90 = (s32[2]{0:T(128)S(1)}, s32[2]{0:T(128)}, u32[]{:S(2)}) copy-start(s32[2]{0:T(128)} %copy-done.89) | copy-start | bytes 28 | tf_op jit(solution)/shard_map/while
  688.0 12.2 %copy-start.10 = (bf16[2,128,8,128]{3,1,2,0:T(8,128)(2,1)S(1)}, bf16[2,128,8,128]{3,1,2,0:T(8,128)(2,1)}, u32[]{:S(2)}) copy-start(bf16[2,128,8,128]{3,1,2,0:T(8,128)(2,1)} %copy-done.9) | copy-start | bytes 1572868 | tf_op jit(solution)/shard_map/while
  688.0 12.2 %copy-start.59 = (f32[2,8,2,128]{3,0,1,2:T(2,128)S(1)}, f32[2,8,2,128]{3,0,1,2:T(2,128)}, u32[]{:S(2)}) copy-start(f32[2,8,2,128]{3,0,1,2:T(2,128)} %copy-done.58) | copy-start | bytes 49156 | tf_op jit(solution)/shard_map/while
  688.0 12.2 %copy-start.63 = (f32[2,8,2,128]{3,2,1,0:T(2,128)S(1)}, f32[2,8,2,128]{3,2,1,0:T(2,128)}, u32[]{:S(2)}) copy-start(f32[2,8,2,128]{3,2,1,0:T(2,128)} %copy-done.62) | copy-start | bytes 49156 | tf_op jit(solution)/shard_map/while
  688.0 12.2 %copy-start.88 = (pred[2,128]{1,0:T(4,128)(4,1)S(1)}, pred[2,128]{1,0:T(4,128)(4,1)}, u32[]{:S(2)}) copy-start(pred[2,128]{1,0:T(4,128)(4,1)} %copy-done.87) | copy-start | bytes 772 | tf_op jit(solution)/shard_map/while
  688.0 12.2 %copy-start.90 = (s32[2]{0:T(128)S(1)}, s32[2]{0:T(128)}, u32[]{:S(2)}) copy-start(s32[2]{0:T(128)} %copy-done.89) | copy-start | bytes 28 | tf_op jit(solution)/shard_map/while
  709.2 211.7 %reduce-scatter.3.cloned.1.call-start = ((), (), s32[]{:S(2)}) async-start(), calls=%async_computation.4 | async-start | bytes 8912896 | tf_op jit(solution)/shard_map/reduce_scatter | solution.py:621
  725.5 10.6 slice-start.2
  1110.4 13.9 %copy-start.55 = (bf16[2,2,16,3072]{3,2,1,0:T(8,128)(2,1)S(1)}, bf16[2,2,16,3072]{3,2,1,0:T(8,128)(2,1)}, u32[]{:S(2)}) copy-start(bf16[2,2,16,3072]{3,2,1,0:T(8,128)(2,1)} %get-tuple-element.201) | copy-start | bytes 1179652
  1110.4 14.9 %copy-start.54 = (bf16[2,2,16,3072]{3,2,1,0:T(8,128)(2,1)S(1)}, bf16[2,2,16,3072]{3,2,1,0:T(8,128)(2,1)}, u32[]{:S(2)}) copy-start(bf16[2,2,16,3072]{3,2,1,0:T(8,128)(2,1)} %get-tuple-element.202) | copy-start | bytes 1179652
  1117.3 8.9 copy-start.53
  (95 other events, 329.9 us)
Sparse Core Ops, SparseCore 0:
  193.9 86.3 all-gather.4
  283.1 76.2 all-gather.2
  709.3 103.0 reduce-scatter.4
  816.2 104.5 reduce-scatter.2

commit v2 on v1

v2 whole, which is shorter than its diff:
```python
from functools import partial

import jax
import jax.numpy as jnp
from jax import lax
from jax.experimental import pallas as pl
from jax.experimental.pallas import tpu as pltpu
from jax.sharding import PartitionSpec as P

MODEL_WIDTH = 1024
QUERY_HEADS = 16
KEY_VALUE_HEADS = 8
HEAD_SIZE = 128
PROMPT_LENGTH = 1024
CONT = 8
CONTINUATION_LEN = 128

norm_epsilon = 1e-06
rope_theta = 1000000.0
masked_score = -1e30
MESH = pl.DeviceIdType.MESH
bf16 = jnp.bfloat16
f32 = jnp.float32

def position(n):
    rep = lax.axis_index("rep")
    rank = lax.axis_index("fsdp")
    return rep, rank // 4, (rank // 2) % 2, rank % 2


def meet(peers):
    barrier = pltpu.get_barrier_semaphore()
    for p in peers:
        pl.semaphore_signal(barrier, inc=1, device_id=p, device_id_type=MESH)
    pl.semaphore_wait(barrier, len(peers))


def remote(src, dst, send, recv, to):
    return pltpu.make_async_remote_copy(src, dst, send, recv, device_id=to, device_id_type=MESH)


def gather_kernel(n, m, k, *refs):
    A = n // 4
    it = iter(refs)
    take = lambda count: [next(it) for _ in range(count)]
    own, (tile,), pieces = take(m), take(1), take(k)
    full, (tiles,), staged = take(m), take(1), take(k)
    zs, zr, s2s, s2r, s3s, s3r, cs, cr, ls, ts, tr, ps, pr, pls = take(14)
    rep, a, b, c = position(n)
    me = (a * 2 + b) * 2 + c
    h = rep % 2
    mate = rep + 1 - 2 * h

    def dev(r, a, b, c):
        return (r, (a * 2 + b) * 2 + c)

    meet([(rep, (me + d) % n) for d in range(1, n)] + [dev(mate, a, b, c)])
    ydev, xdev, cdev = dev(rep, a, 1 - b, c), dev(mate, a, b, c), dev(rep, a, b, 1 - c)

    def local(i):
        return pltpu.make_async_copy(own[i].at[:, h], full[i].at[a, b, c, :, h], ls.at[i])

    def along(i, d):
        return remote(own[i].at[:, h], full[i].at[a, b, c, :, h], zs.at[i, d - 1], zr.at[i, d - 1], dev(rep, (a + d) % A, b, c))

    def s2(i):
        y, x = full[i].at[:, b, c, 0, h], full[i].at[:, b, c, 1, h]
        return [remote(y, y, s2s.at[i, 0], s2r.at[i, 0], ydev), remote(x, x, s2s.at[i, 1], s2r.at[i, 1], xdev)]

    def s3(i):
        x, y = full[i].at[:, :, c, 0, h], full[i].at[:, b, c, 1]
        return [remote(x, x, s3s.at[i, 0], s3r.at[i, 0], xdev), remote(y, y, s3s.at[i, 1], s3r.at[i, 1], ydev)]

    def s4(i):
        both = full[i].at[:, :, c]
        return [remote(both, both, cs.at[i], cr.at[i], cdev)]

    def share(d):
        return remote(tile, tiles.at[me], ts.at[d - 1], tr.at[d - 1], (rep, (me + d) % n))

    def piece(i, d):
        to = (me + d) % n
        return remote(pieces[i].at[:, to], staged[i].at[me], ps.at[i, d - 1], pr.at[i, d - 1], (rep, to))

    def own_piece(i):
        return pltpu.make_async_copy(pieces[i].at[:, me], staged[i].at[me], pls.at[i])

    for d in range(1, n):
        share(d).start()
    tiles[me] = tile[...]
    for i in range(k):
        own_piece(i).start()
        for d in range(1, n):
            piece(i, d).start()
    for i in range(m):
        local(i).start()
        for d in range(1, A):
            along(i, d).start()
    for t in range(m + 3):
        if t < m:
            local(t).wait()
            for d in range(1, A):
                along(t, d).wait_recv()
            for q in s2(t):
                q.start()
        if 0 <= t - 1 < m:
            for q in s2(t - 1):
                q.wait_recv()
            for q in s3(t - 1):
                q.start()
        if 0 <= t - 2 < m:
            for q in s3(t - 2):
                q.wait_recv()
            for q in s4(t - 2):
                q.start()
        if 0 <= t - 3 < m:
            for q in s4(t - 3):
                q.wait_recv()
    for d in range(1, n):
        share(d).wait()
    for i in range(k):
        own_piece(i).wait()
        for d in range(1, n):
            piece(i, d).wait()
    for t in range(m):
        for d in range(1, A):
            along(t, d).wait_send()
        for q in s2(t) + s3(t) + s4(t):
            q.wait_send()


def gather(shards, tile, slots, n, cid):
    m, k, A = len(shards), len(slots), n // 4
    views = [s.reshape(2, 2, s.shape[0] // 4, s.shape[1]) for s in shards]
    outs = [jax.ShapeDtypeStruct((A, 2, 2) + v.shape, v.dtype) for v in views]
    outs += [jax.ShapeDtypeStruct((n,) + tile.shape, tile.dtype)]
    outs += [jax.ShapeDtypeStruct((n, s.shape[0]) + s.shape[2:], s.dtype) for s in slots]
    D = pltpu.SemaphoreType.DMA
    vm, hbm = pl.BlockSpec(memory_space=pltpu.VMEM), pl.BlockSpec(memory_space=pl.ANY)
    res = pl.pallas_call(
        partial(gather_kernel, n, m, k),
        out_shape=outs,
        in_specs=[vm] * (m + 1 + k),
        out_specs=[hbm] * m + [vm] + [hbm] * k,
        scratch_shapes=[D((m, A - 1))] * 2 + [D((m, 2))] * 4 + [D((m,))] * 3 + [D((n - 1,))] * 2 + [D((max(k, 1), n - 1))] * 2 + [D((max(k, 1),))],
        compiler_params=pltpu.CompilerParams(collective_id=cid, has_side_effects=True),
        name="gather",
    )(*views, tile, *slots)
    return [f.reshape(-1, s.shape[1]) for f, s in zip(res, shards)], res[m], res[m + 1:]


def spread_kernel(n, k, *refs):
    it = iter(refs)
    take = lambda count: [next(it) for _ in range(count)]
    pieces, staged, (ps, pr, pls) = take(k), take(k), take(3)
    rep, a, b, c = position(n)
    me = (a * 2 + b) * 2 + c
    meet([(rep, (me + d) % n) for d in range(1, n)])

    def piece(i, d):
        to = (me + d) % n
        return remote(pieces[i].at[:, to], staged[i].at[me], ps.at[i, d - 1], pr.at[i, d - 1], (rep, to))

    def own_piece(i):
        return pltpu.make_async_copy(pieces[i].at[:, me], staged[i].at[me], pls.at[i])

    for i in range(k):
        own_piece(i).start()
        for d in range(1, n):
            piece(i, d).start()
    for i in range(k):
        own_piece(i).wait()
        for d in range(1, n):
            piece(i, d).wait()


def spread(slots, n, cid):
    k = len(slots)
    D = pltpu.SemaphoreType.DMA
    vm, hbm = pl.BlockSpec(memory_space=pltpu.VMEM), pl.BlockSpec(memory_space=pl.ANY)
    return pl.pallas_call(
        partial(spread_kernel, n, k),
        out_shape=[jax.ShapeDtypeStruct((n, s.shape[0]) + s.shape[2:], s.dtype) for s in slots],
        in_specs=[vm] * k,
        out_specs=[hbm] * k,
        scratch_shapes=[D((k, n - 1))] * 2 + [D((k,))],
        compiler_params=pltpu.CompilerParams(collective_id=cid, has_side_effects=True),
        name="spread",
    )(*slots)


def collect_kernel(n, k, *refs):
    it = iter(refs)
    take = lambda count: [next(it) for _ in range(count)]
    (index,), staged, final, ordered, (ps, pr, pls) = take(1), take(k), take(k), take(k), take(3)
    rep, a, b, c = position(n)
    me = (a * 2 + b) * 2 + c
    meet([(rep, (me + d) % n) for d in range(1, n)])
    S = ordered[0].shape[1]
    for i in range(k):
        def place(j, _):
            ordered[i][j // S, j % S] = staged[i][index[j]]
            return 0
        lax.fori_loop(0, n * S, place, 0)

    def piece(i, d):
        to = (me + d) % n
        return remote(ordered[i].at[to], final[i].at[:, me], ps.at[i, d - 1], pr.at[i, d - 1], (rep, to))

    def own_piece(i):
        return pltpu.make_async_copy(ordered[i].at[me], final[i].at[:, me], pls.at[i])

    for i in range(k):
        own_piece(i).start()
        for d in range(1, n):
            piece(i, d).start()
    for i in range(k):
        own_piece(i).wait()
        for d in range(1, n):
            piece(i, d).wait()


def collect(index, staged, n, cid):
    k = len(staged)
    flat = [s.reshape((-1,) + s.shape[2:]) for s in staged]
    D = pltpu.SemaphoreType.DMA
    vm, hbm, sm = pl.BlockSpec(memory_space=pltpu.VMEM), pl.BlockSpec(memory_space=pl.ANY), pl.BlockSpec(memory_space=pltpu.SMEM)
    return pl.pallas_call(
        partial(collect_kernel, n, k),
        out_shape=[jax.ShapeDtypeStruct((s.shape[1], n) + s.shape[2:], s.dtype) for s in staged],
        in_specs=[sm] + [vm] * k,
        out_specs=[hbm] * k,
        scratch_shapes=[pltpu.VMEM(s.shape, s.dtype) for s in staged] + [D((k, n - 1))] * 2 + [D((k,))],
        compiler_params=pltpu.CompilerParams(collective_id=cid, has_side_effects=True),
        name="collect",
    )(index, *flat)


def add_rows(count, out, first, second, step=None):
    def one(j, _):
        o = out(j)
        total = first(j)[...].astype(jnp.float32)
        for s in second:
            total = total + s(j)[...].astype(jnp.float32)
        o[...] = total.astype(o.dtype)
        return 0
    lax.fori_loop(0, count, one, 0)

def scatter_kernel(n, R, m, has_vec, *refs):
    A = n // 4
    bits = R.bit_length() - 1
    it = iter(refs)
    take = lambda k: [next(it) for _ in range(k)]
    grads = take(m)
    vec = next(it) if has_vec else None
    outs = take(m)
    vout = next(it) if has_vec else None
    own, b1, b2y, b2x, b3, b4, b5 = [take(m) for _ in range(7)]
    s4 = take(m)
    vb = next(it) if has_vec else None
    vz = next(it) if has_vec else None
    ls, s1s, s1r, s2s, s2r, s3s, s3r, s4s, s4r, s5s, s5r, ws = take(12)
    if has_vec:
        vs, vr = take(2)
    rep, a, b, c = position(n)
    h = rep % 2
    mate = rep + 1 - 2 * h
    def dev(r, a, b, c):
        return (r, (a * 2 + b) * 2 + c)
    ydev, xdev, cdev = dev(rep, a, 1 - b, c), dev(mate, a, b, c), dev(rep, a, b, 1 - c)
    zdev = lambda d: dev(rep, (a + d) % A, b, c)
    def flip(bit):
        w = 1 << bit
        return dev(rep + w - 2 * w * ((rep // w) % 2), a, b, c)
    barrier = pltpu.get_barrier_semaphore()
    peers = [zdev(d) for d in range(1, A)] + [ydev, xdev, cdev] + [flip(k) for k in range(1, bits)]
    for p in peers:
        pl.semaphore_signal(barrier, inc=1, device_id=p, device_id_type=MESH)
    pl.semaphore_wait(barrier, len(peers))
    def rc(src, dst, ss, rs, to):
        return pltpu.make_async_remote_copy(src, dst, ss, rs, device_id=to, device_id_type=MESH)
    def load(i): return pltpu.make_async_copy(grads[i].at[:, :, c], own[i], ls.at[i])
    def S1(i): return [rc(grads[i].at[:, :, 1 - c], b1[i], s1s.at[i], s1r.at[i], cdev)]
    def S2(i): return [rc(b1[i].at[:, 1 - b, 0], b2y[i], s2s.at[i, 0], s2r.at[i, 0], ydev),
                       rc(b1[i].at[:, :, 1, 1 - h], b2x[i], s2s.at[i, 1], s2r.at[i, 1], xdev)]
    def S3(i): return [rc(b2y[i].at[:, 1 - h], b3[i].at[0], s3s.at[i, 0], s3r.at[i, 0], xdev),
                       rc(b2x[i].at[:, 1 - b], b3[i].at[1], s3s.at[i, 1], s3r.at[i, 1], ydev)]
    def S4(i): return [rc(b3[i].at[:, (a + d) % A], b4[i].at[d - 1], s4s.at[i, d - 1], s4r.at[i, d - 1], zdev(d)) for d in range(1, A)]
    def S5(i, k): return rc(s4[i].at[0] if k == bits - 1 else s4[i].at[k], b5[i].at[k], s5s.at[i, k], s5r.at[i, k], xdev if k == bits - 1 else flip(k + 1))
    def put(i, k): return pltpu.make_async_copy((s4[i].at[0] if bits == 1 else s4[i].at[bits - 1]) if k == 0 else b5[i].at[bits - 1], outs[i].at[:, h if k == 0 else 1 - h], ws.at[i, k])
    for i in range(m):
        load(i).start()
        for q in S1(i): q.start()
    if has_vec:
        rounds = [cdev, ydev, xdev] + [flip(k) for k in range(1, bits)]
        vb[0] = vec[...]
        for k, to in enumerate(rounds):
            q = rc(vb.at[2 * k], vb.at[2 * k + 1], vs.at[k], vr.at[k], to)
            q.start(); q.wait()
            vb[2 * k + 2] = vb[2 * k] + vb[2 * k + 1]
        last = 2 * len(rounds)
        nr = len(rounds)
        qs = [rc(vb.at[last], vz.at[a], vs.at[nr + d - 1], vr.at[nr + d - 1], zdev(d)) for d in range(1, A)]
        for q in qs: q.start()
        vz[a] = vb[last]
        for q in qs: q.wait()
        total = vz[0]
        for k in range(1, A):
            total = total + vz[k]
        vout[...] = total
    for t in range(m + 4):
        i = t
        if t < m:
            load(i).wait()
            for q in S1(i): q.wait_recv()
            add_rows(A * 2 * 4, lambda j, i=i: b1[i].at[j // 8, (j // 4) % 2, (j // 2) % 2, j % 2],
                     lambda j, i=i: b1[i].at[j // 8, (j // 4) % 2, (j // 2) % 2, j % 2],
                     [lambda j, i=i: own[i].at[j // 8, (j // 4) % 2, (j // 2) % 2, j % 2]])
            for q in S2(i): q.start()
        i = t - 1
        if 0 <= i < m:
            for q in S2(i): q.wait_recv()
            add_rows(A * 2, lambda j, i=i: b2y[i].at[j // 2, j % 2], lambda j, i=i: b2y[i].at[j // 2, j % 2],
                     [lambda j, i=i: b1[i].at[j // 2, b, 0, j % 2]])
            add_rows(A * 2, lambda j, i=i: b2x[i].at[j // 2, j % 2], lambda j, i=i: b2x[i].at[j // 2, j % 2],
                     [lambda j, i=i: b1[i].at[j // 2, j % 2, 1, h]])
            for q in S3(i): q.start()
        i = t - 2
        if 0 <= i < m:
            for q in S3(i): q.wait_recv()
            add_rows(A, lambda j, i=i: b3[i].at[0, j], lambda j, i=i: b3[i].at[0, j], [lambda j, i=i: b2y[i].at[j, h]])
            add_rows(A, lambda j, i=i: b3[i].at[1, j], lambda j, i=i: b3[i].at[1, j], [lambda j, i=i: b2x[i].at[j, b]])
            for q in S4(i): q.start()
        i = t - 3
        if 0 <= i < m:
            for q in S4(i): q.wait_recv()
            add_rows(2, lambda j, i=i: s4[i].at[0, j], lambda j, i=i: b3[i].at[j, a], [lambda j, i=i, d=d: b4[i].at[d, j] for d in range(A - 1)])
            for k in range(bits - 1):
                q = S5(i, k); q.start(); q.wait()
                add_rows(2, lambda j, i=i, k=k: s4[i].at[k + 1, j], lambda j, i=i, k=k: s4[i].at[k, j], [lambda j, i=i, k=k: b5[i].at[k, j]])
            rc(s4[i].at[bits - 1], b5[i].at[bits - 1], s5s.at[i, bits - 1], s5r.at[i, bits - 1], xdev).start()
            put(i, 0).start()
        i = t - 4
        if 0 <= i < m:
            rc(s4[i].at[bits - 1], b5[i].at[bits - 1], s5s.at[i, bits - 1], s5r.at[i, bits - 1], xdev).wait_recv()
            put(i, 1).start()
    for i in range(m):
        for q in S1(i) + S2(i) + S3(i) + S4(i): q.wait_send()
        rc(s4[i].at[bits - 1], b5[i].at[bits - 1], s5s.at[i, bits - 1], s5r.at[i, bits - 1], xdev).wait_send()
        put(i, 0).wait(); put(i, 1).wait()

def scatter(grads, n, R, cid, vec=None):
    m, A, bits = len(grads), n // 4, R.bit_length() - 1
    views = [g.reshape(A, 2, 2, 2, 2, g.shape[0] // (4 * n), g.shape[1]) for g in grads]
    sub = [v.shape[-2:] for v in views]
    bf = jnp.bfloat16
    V, D = pltpu.VMEM, pltpu.SemaphoreType.DMA
    scratch = ([V((A, 2, 2, 2) + s, bf) for s in sub] * 2 + [V((A, 2) + s, bf) for s in sub] * 2 + [V((2, A) + s, bf) for s in sub]
        + [V((A - 1, 2) + s, bf) for s in sub] + [V((bits, 2) + s, bf) for s in sub] + [V((bits, 2) + s, bf) for s in sub])
    ins, ispec = list(views), [pl.BlockSpec(memory_space=pl.ANY)] * m
    outs, ospec = [jax.ShapeDtypeStruct((2, 2) + s, bf) for s in sub], [pl.BlockSpec(memory_space=pl.ANY)] * m
    sems = [D((m,)), D((m,)), D((m,)), D((m, 2)), D((m, 2)), D((m, 2)), D((m, 2)), D((m, A - 1)), D((m, A - 1)), D((m, bits)), D((m, bits)), D((m, 2))]
    if vec is not None:
        ins.append(vec); ispec.append(pl.BlockSpec(memory_space=pltpu.VMEM))
        outs.append(jax.ShapeDtypeStruct(vec.shape, vec.dtype)); ospec.append(pl.BlockSpec(memory_space=pltpu.VMEM))
        scratch += [V((2 * (2 + bits) + 1,) + vec.shape, vec.dtype), V((A,) + vec.shape, vec.dtype)]
        sems += [D((2 + bits + A - 1,))] * 2
    res = pl.pallas_call(partial(scatter_kernel, n, R, m, vec is not None), out_shape=outs, in_specs=ispec, out_specs=ospec,
        scratch_shapes=scratch + sems,
        compiler_params=pltpu.CompilerParams(collective_id=cid, has_side_effects=True, vmem_limit_bytes=60 << 20),
        name="scatter")(*ins)
    shards = [r.reshape(-1, r.shape[-1]) for r in res[:m]]
    return (shards, res[m]) if vec is not None else shards


LOG2E = 1.4426950408889634


def mm(x, y, cx, cy):
    return lax.dot_general(x, y, (((cx,), (cy,)), ((), ())), preferred_element_type=f32)


def keys_kernel(n, group, k_pre, v, gain, cos, sin, k_out, ks, vs, fs, fr, gs, gr, ls):
    rows = ks.shape[2]
    half = group // 2
    rep, a, b, c = position(n)
    me = (a * 2 + b) * 2 + c
    first = (me // group) * half
    slot = (me // 2) % half

    def at(s, c):
        return (rep, (first + s) * 2 + c)

    others = [(slot + d) % half for d in range(1, half)]
    meet([at(s, c) for s in others] + [at(slot, 1 - c)])

    def head(j, _):
        lanes = pl.ds(pl.multiple_of(j * HEAD_SIZE, HEAD_SIZE), HEAD_SIZE)
        x = k_pre[:, lanes]
        x = x * lax.rsqrt(jnp.mean(x * x, axis=-1, keepdims=True) + norm_epsilon) * gain[...]
        k_out[:, lanes] = (x * cos[...] + pltpu.roll(x, HEAD_SIZE // 2, 1) * sin[...]).astype(bf16)
        return 0

    lax.fori_loop(0, KEY_VALUE_HEADS, head, 0)
    parts = [(k_out, ks), (v, vs)]

    def local(i):
        return pltpu.make_async_copy(parts[i][0].at[pl.ds(0, rows)], parts[i][1].at[slot, c], ls.at[i])

    def across(i, d):
        return remote(parts[i][0].at[pl.ds(0, rows)], parts[i][1].at[slot, c], fs.at[i, d - 1], fr.at[i, d - 1], at((slot + d) % half, c))

    def sibling(i, d):
        if d == 0:
            return remote(parts[i][0].at[pl.ds(0, rows)], parts[i][1].at[slot, c], gs.at[i, d], gr.at[i, d], at(slot, 1 - c))
        there = parts[i][1].at[(slot + half - d) % half, c]
        return remote(there, there, gs.at[i, d], gr.at[i, d], at(slot, 1 - c))

    for i in range(2):
        for d in range(1, half):
            across(i, d).start()
        sibling(i, 0).start()
        local(i).start()
    for i in range(2):
        for d in range(1, half):
            across(i, d).wait_recv()
            sibling(i, d).start()
    for i in range(2):
        local(i).wait()
        sibling(i, 0).wait()
        for d in range(1, half):
            across(i, d).wait_send()
            sibling(i, d).wait()


def gather_keys(k_pre, v, gain, cos, sin, rows, n, cid):
    group = PROMPT_LENGTH // rows
    half = group // 2
    width = k_pre.shape[1]
    D = pltpu.SemaphoreType.DMA
    vm, hbm = pl.BlockSpec(memory_space=pltpu.VMEM), pl.BlockSpec(memory_space=pl.ANY)
    wide = jax.ShapeDtypeStruct((half, 2, rows, width), bf16)
    k_rot, ks, vs = pl.pallas_call(
        partial(keys_kernel, n, group),
        out_shape=[jax.ShapeDtypeStruct(k_pre.shape, bf16), wide, wide],
        in_specs=[vm] * 5,
        out_specs=[vm, hbm, hbm],
        scratch_shapes=[D((2, max(half - 1, 1)))] * 2 + [D((2, half))] * 2 + [D((2,))],
        compiler_params=pltpu.CompilerParams(collective_id=cid, has_side_effects=True),
        name="prompt_keys",
    )(k_pre, v, gain, cos, sin)
    return k_rot, ks.reshape(PROMPT_LENGTH, width), vs.reshape(PROMPT_LENGTH, width)


def key_grads_kernel(n, group, dk, dv, dks, dvs, k_pre, gain, cos, sin, dk_out, dv_out, g_out, s1, r1, s2, r2, dk_rot, gs, gr, fs, fr):
    rows = dk.shape[2]
    half = group // 2
    rep, a, b, c = position(n)
    me = (a * 2 + b) * 2 + c
    first = (me // group) * half
    slot = (me // 2) % half

    def at(s, c):
        return (rep, (first + s) * 2 + c)

    meet([at((slot + d) % half, c) for d in range(1, half)] + [at(slot, 1 - c)])
    parts = [dk, dv]

    def to_sibling(i, d):
        s = (slot + d) % half
        return remote(parts[i].at[s, 1 - c], r1.at[i, d], gs.at[i, d], gr.at[i, d], at(slot, 1 - c))

    def across(i, d):
        return remote(s1.at[i, d], r2.at[i, d - 1], fs.at[i, d - 1], fr.at[i, d - 1], at((slot + d) % half, c))

    order = list(range(1, half)) + [0]
    for d in order:
        for i in range(2):
            to_sibling(i, d).start()
    for d in order:
        for i in range(2):
            to_sibling(i, d).wait_recv()
            s1[i, d] = (parts[i][(slot + d) % half, c].astype(f32) + r1[i, d].astype(f32)).astype(bf16)
            if d:
                across(i, d).start()
    for i in range(2):
        for d in range(1, half):
            across(i, d).wait_recv()

    def total(i):
        t = s1[i, 0].astype(f32)
        for d in range(1, half):
            t = t + r2[i, d - 1].astype(f32)
        return t

    dv_out[pl.ds(0, rows), :] = total(1).astype(bf16)
    dv_out[pl.ds(rows, dvs.shape[0]), :] = dvs[...].astype(bf16)
    dk_rot[pl.ds(0, rows), :] = total(0)
    dk_rot[pl.ds(rows, dks.shape[0]), :] = dks[...].astype(f32)
    g_out[...] = jnp.zeros_like(g_out)

    def head(j, _):
        lanes = pl.ds(pl.multiple_of(j * HEAD_SIZE, HEAD_SIZE), HEAD_SIZE)
        x = k_pre[:, lanes]
        rs = lax.rsqrt(jnp.mean(x * x, axis=-1, keepdims=True) + norm_epsilon)
        unit = x * rs
        dy = dk_rot[:, lanes]
        dy = dy * cos[...] - pltpu.roll(dy, HEAD_SIZE // 2, 1) * sin[...]
        g_out[0:1, :] += jnp.sum(dy * unit, axis=0, keepdims=True)
        dy = dy * gain[...]
        dk_out[:, lanes] = (rs * (dy - unit * jnp.mean(dy * unit, axis=-1, keepdims=True))).astype(bf16)
        return 0

    lax.fori_loop(0, KEY_VALUE_HEADS, head, 0)
    for i in range(2):
        for d in range(half):
            to_sibling(i, d).wait_send()
            if d:
                across(i, d).wait_send()


def key_grads(dk, dv, dks, dvs, k_pre, gain, cos, sin, rows, n, cid):
    group = PROMPT_LENGTH // rows
    half = group // 2
    width = k_pre.shape[1]
    D = pltpu.SemaphoreType.DMA
    vm = pl.BlockSpec(memory_space=pltpu.VMEM)
    V = pltpu.VMEM
    block = (rows, width)
    return pl.pallas_call(
        partial(key_grads_kernel, n, group),
        out_shape=[jax.ShapeDtypeStruct(k_pre.shape, bf16), jax.ShapeDtypeStruct(k_pre.shape, bf16), jax.ShapeDtypeStruct((8, HEAD_SIZE), f32)],
        in_specs=[vm] * 8,
        out_specs=[vm] * 3,
        scratch_shapes=[V((2, half) + block, bf16), V((2, half) + block, bf16), V((1, 8, 128), bf16), V((2, max(half - 1, 1)) + block, bf16), V(k_pre.shape, f32)]
        + [D((2, half))] * 2 + [D((2, max(half - 1, 1)))] * 2,
        compiler_params=pltpu.CompilerParams(collective_id=cid, has_side_effects=True, vmem_limit_bytes=60 << 20),
        name="prompt_key_grads",
    )(dk.reshape(half, 2, rows, width), dv.reshape(half, 2, rows, width), dks, dvs, k_pre, gain, cos, sin)


def attend_kernel(rows, q_pre, ks, vs, k_own, v_own, gain, cos, sin, past, inside, out, q_out, lse_out, rs_out):
    scale = HEAD_SIZE ** -0.5 * LOG2E
    for g in range(QUERY_HEADS // KEY_VALUE_HEADS):
        lanes = slice(g * HEAD_SIZE, (g + 1) * HEAD_SIZE)
        q = q_pre[:, lanes].T
        rs = lax.rsqrt(jnp.mean(q * q, axis=0, keepdims=True) + norm_epsilon)
        rs_out[0, g:g + 1, :] = rs
        q = q * rs * gain[:, 0:1]
        lo, hi = q[:HEAD_SIZE // 2], q[HEAD_SIZE // 2:]
        q = jnp.concatenate([lo * cos[...] - hi * sin[...], hi * cos[...] + lo * sin[...]], axis=0).astype(bf16)
        q_out[lanes, :] = q
        p = jnp.exp2(mm(ks[...], q[:, :rows], 1, 0) * scale + past[...])
        total = jnp.sum(p, axis=0, keepdims=True)
        o = mm(vs[...], p.astype(bf16), 0, 0) / total
        out[:rows, lanes] = o.T.astype(bf16)
        lse_out[0, g:g + 1, :rows] = jnp.log2(total)
        p = jnp.exp2(mm(ks[...], q[:, rows:], 1, 0) * scale)
        r = jnp.exp2(mm(k_own[rows:, :], q[:, rows:], 1, 0) * scale + inside[...])
        total = jnp.sum(p, axis=0, keepdims=True) + jnp.sum(r, axis=0, keepdims=True)
        o = (mm(vs[...], p.astype(bf16), 0, 0) + mm(v_own[rows:, :], r.astype(bf16), 0, 0)) / total
        out[rows:, lanes] = o.T.astype(bf16)
        lse_out[0, g:g + 1, rows:] = jnp.log2(total)


def attend(q_pre, ks, vs, k_own, v_own, gain, cos, sin, past, inside, rows):
    total = q_pre.shape[0]
    pair = 2 * HEAD_SIZE
    whole = lambda x: pl.BlockSpec(x.shape, lambda j: (0,) * x.ndim)
    col = lambda r, w: pl.BlockSpec((r, w), lambda j: (0, j))
    small = pl.BlockSpec((1, 2, total), lambda j: (j, 0, 0))
    return pl.pallas_call(
        partial(attend_kernel, rows),
        grid=(KEY_VALUE_HEADS,),
        in_specs=[col(total, pair), col(PROMPT_LENGTH, HEAD_SIZE), col(PROMPT_LENGTH, HEAD_SIZE), col(total, HEAD_SIZE), col(total, HEAD_SIZE),
                  whole(gain), whole(cos), whole(sin), whole(past), whole(inside)],
        out_specs=[col(total, pair), pl.BlockSpec((pair, total), lambda j: (j, 0)), small, small],
        out_shape=[jax.ShapeDtypeStruct((total, QUERY_HEADS * HEAD_SIZE), bf16), jax.ShapeDtypeStruct((QUERY_HEADS * HEAD_SIZE, total), bf16),
                   jax.ShapeDtypeStruct((KEY_VALUE_HEADS, 2, total), f32), jax.ShapeDtypeStruct((KEY_VALUE_HEADS, 2, total), f32)],
        compiler_params=pltpu.CompilerParams(vmem_limit_bytes=60 << 20),
        name="attend",
    )(q_pre, ks, vs, k_own, v_own, gain, cos, sin, past, inside)


def attend_back_kernel(rows, q_rot, ks, vs, k_own, v_own, d_out, out, lse, rs_in, gain, cos, sin, past, inside, dq_out, dk_out, dv_out, dks_out, dvs_out, g_out):
    scale = HEAD_SIZE ** -0.5
    dk = dv = dks = dvs = None
    plus = lambda x, y: y if x is None else x + y
    gain_grad = None
    for g in range(QUERY_HEADS // KEY_VALUE_HEADS):
        lanes = slice(g * HEAD_SIZE, (g + 1) * HEAD_SIZE)
        q = q_rot[lanes, :]
        do = d_out[:, lanes]
        delta = jnp.sum((do.astype(f32) * out[:, lanes].astype(f32)).T, axis=0, keepdims=True)
        log_total = lse[0, g:g + 1, :]
        dq = []
        for suffix in range(2):
            part = slice(rows, None) if suffix else slice(0, rows)
            qp, dop, lp, dp = q[:, part], do[part], log_total[:, part], delta[:, part]
            blocks = [(ks[...], vs[...], None if suffix else past[...])]
            if suffix:
                blocks.append((k_own[rows:, :], v_own[rows:, :], inside[...]))
            dqp = None
            for i, (kb, vb, bias) in enumerate(blocks):
                s = mm(kb, qp, 1, 0) * (scale * LOG2E) - lp
                p = jnp.exp2(s if bias is None else s + bias)
                ds = (p * (mm(vb, dop, 1, 1) - dp)).astype(bf16)
                dvp = mm(p.astype(bf16), dop, 1, 0)
                dkp = mm(ds, qp, 1, 1)
                dqp = plus(dqp, mm(kb, ds, 0, 0))
                if i:
                    dks, dvs = plus(dks, dkp), plus(dvs, dvp)
                else:
                    dk, dv = plus(dk, dkp), plus(dv, dvp)
            dq.append(dqp)
        dq = jnp.concatenate(dq, axis=1) * scale
        half = HEAD_SIZE // 2
        c, s = cos[...], sin[...]
        dy = jnp.concatenate([dq[:half] * c + dq[half:] * s, dq[half:] * c - dq[:half] * s], axis=0)
        qf = q.astype(f32)
        unit = jnp.concatenate([qf[:half] * c + qf[half:] * s, qf[half:] * c - qf[:half] * s], axis=0) / gain[:, 0:1]
        gg = dy * unit
        for t in range(gg.shape[1] // 128):
            gain_grad = plus(gain_grad, gg[:, t * 128:(t + 1) * 128])
        dy = dy * gain[:, 0:1]
        dx = rs_in[0, g:g + 1, :] * (dy - unit * jnp.mean(dy * unit, axis=0, keepdims=True))
        dq_out[:, lanes] = dx.T.astype(bf16)
    dk_out[...] = (dk * scale).astype(bf16)
    dv_out[...] = dv.astype(bf16)
    dks_out[...] = (dks * scale).astype(bf16)
    dvs_out[...] = dvs.astype(bf16)

    @pl.when(pl.program_id(0) == 0)
    def _():
        g_out[...] = gain_grad

    @pl.when(pl.program_id(0) > 0)
    def _():
        g_out[...] += gain_grad


def attend_back(q_rot, ks, vs, k_own, v_own, d_out, out, lse, rs, gain, cos, sin, past, inside, rows):
    total = k_own.shape[0]
    pair = 2 * HEAD_SIZE
    whole = lambda x: pl.BlockSpec(x.shape, lambda j: (0,) * x.ndim)
    col = lambda r, w: pl.BlockSpec((r, w), lambda j: (0, j))
    small = pl.BlockSpec((1, 2, total), lambda j: (j, 0, 0))
    width = KEY_VALUE_HEADS * HEAD_SIZE
    kv, own = jax.ShapeDtypeStruct((PROMPT_LENGTH, width), bf16), jax.ShapeDtypeStruct((total - rows, width), bf16)
    return pl.pallas_call(
        partial(attend_back_kernel, rows),
        grid=(KEY_VALUE_HEADS,),
        in_specs=[pl.BlockSpec((pair, total), lambda j: (j, 0)), col(PROMPT_LENGTH, HEAD_SIZE), col(PROMPT_LENGTH, HEAD_SIZE), col(total, HEAD_SIZE),
                  col(total, HEAD_SIZE), col(total, pair), col(total, pair), small, small, whole(gain), whole(cos), whole(sin), whole(past), whole(inside)],
        out_specs=[col(total, pair), col(PROMPT_LENGTH, HEAD_SIZE), col(PROMPT_LENGTH, HEAD_SIZE), col(total - rows, HEAD_SIZE), col(total - rows, HEAD_SIZE),
                   pl.BlockSpec((HEAD_SIZE, 128), lambda j: (0, 0))],
        out_shape=[jax.ShapeDtypeStruct((total, QUERY_HEADS * HEAD_SIZE), bf16), kv, kv, own, own, jax.ShapeDtypeStruct((HEAD_SIZE, 128), f32)],
        compiler_params=pltpu.CompilerParams(vmem_limit_bytes=60 << 20),
        name="attend_back",
    )(q_rot, ks, vs, k_own, v_own, d_out, out, lse, rs, gain, cos, sin, past, inside)


def root_mean_scale(values, gain_vector):
    return (
        values
        * lax.rsqrt(jnp.mean(values * values, axis=-1, keepdims=True) + norm_epsilon)
        * gain_vector
    )


def swiglu(gate_pre, up_pre):
    return jax.nn.silu(gate_pre) * up_pre


def dot(x, y):
    return jnp.dot(x, y, preferred_element_type=f32)


def dot_tn(x, y):
    return jnp.einsum("ra,rb->ab", x, y, preferred_element_type=f32)


def dot_nt(x, y):
    return jnp.einsum("ra,ba->rb", x, y, preferred_element_type=f32)


def per_device(
    prompt_rows,
    suffix_rows,
    assignment,
    lengths,
    attention_gain,
    query_weight,
    key_matrix,
    value_matrix,
    query_gain,
    key_norm_gain,
    out_weight,
    mlp_gain,
    gate_weight,
    up_weight,
    down_weight,
    prompt_cotangent,
    suffix_cotangent,
):
    n, R = lax.axis_size("fsdp"), lax.axis_size("rep")
    rank = lax.axis_index("fsdp")
    rows = prompt_rows.shape[0]
    suffix = suffix_rows.shape[0]
    S = suffix // CONTINUATION_LEN
    total = rows + suffix
    width = MODEL_WIDTH

    pad = lambda v: jnp.pad(v.astype(f32).reshape(-1), (0, 128 - v.size))
    tile = jnp.stack([pad(v) for v in (attention_gain, mlp_gain, query_gain, key_norm_gain, assignment, lengths)])
    tile = jnp.pad(tile, ((0, 2), (0, 0)))
    cut = lambda v: v.reshape(S, n, CONTINUATION_LEN // n, width)
    weights, tiles, staged = gather(
        [key_matrix, value_matrix, query_weight, out_weight, gate_weight, up_weight, down_weight],
        tile,
        [cut(suffix_rows), cut(suffix_cotangent)],
        n,
        0,
    )
    w_key, w_value, w_query, w_out, w_gate, w_up, w_down = weights
    gain_first = tiles[:, 0, : attention_gain.size].reshape(-1)
    gain_second = tiles[:, 1, : mlp_gain.size].reshape(-1)
    query_scale = tiles[:, 2, : query_gain.size].reshape(-1)
    key_scale = tiles[:, 3, : key_norm_gain.size].reshape(-1)

    owner = tiles[:, 4, :S].reshape(-1).astype(jnp.int32) // CONT
    slot_count = n * S
    ids = jnp.arange(slot_count, dtype=jnp.int32)
    ahead = (owner[None, :] < owner[:, None]) | ((owner[None, :] == owner[:, None]) & (ids[None, :] < ids[:, None]))
    place = jnp.sum(ahead.astype(jnp.int32), axis=1)
    hits = place[None, :] == ids[:, None]
    order = jnp.sum(jnp.where(hits, ids[None, :], 0), axis=1)
    slot_lengths = jnp.sum(jnp.where(hits, tiles[:, 5, :S].reshape(-1).astype(jnp.int32)[None, :], 0), axis=1)
    own_lengths = lax.dynamic_slice_in_dim(slot_lengths, rank * S, S)

    moved_rows, moved_cotangent = [v.reshape(suffix, width) for v in collect(order, staged, n, 1)]

    prompt_place = (rank * rows) % PROMPT_LENGTH + jnp.arange(rows, dtype=jnp.int32)
    suffix_place = jnp.arange(suffix, dtype=jnp.int32) % CONTINUATION_LEN
    suffix_slot = jnp.arange(suffix, dtype=jnp.int32) // CONTINUATION_LEN
    length_rows = jnp.repeat(own_lengths, CONTINUATION_LEN)
    suffix_valid = suffix_place < length_rows
    valid_rows = jnp.concatenate([jnp.ones((rows,), f32), suffix_valid.astype(f32)])
    token_positions = jnp.concatenate([prompt_place, PROMPT_LENGTH + suffix_place]).astype(f32)
    half = HEAD_SIZE // 2
    inverse = rope_theta ** (jnp.arange(half, dtype=f32) * (-2.0 / HEAD_SIZE))
    angles_t = inverse[:, None] * token_positions[None, :]
    cos_t, sin_t = jnp.cos(angles_t), jnp.sin(angles_t)
    cos_r, sin_r = cos_t.T, sin_t.T
    cos_rows = jnp.concatenate([cos_r, cos_r], axis=1)
    sin_rows = jnp.concatenate([-sin_r, sin_r], axis=1)
    past = jnp.where(jnp.arange(PROMPT_LENGTH, dtype=jnp.int32)[:, None] <= prompt_place[None, :], 0.0, masked_score).astype(f32)
    inside = jnp.where(
        (suffix_slot[:, None] == suffix_slot[None, :]) & (suffix_place[:, None] <= suffix_place[None, :]) & suffix_valid[:, None], 0.0, masked_score
    ).astype(f32)

    rows_wide = jnp.concatenate([prompt_rows, moved_rows], 0).astype(f32)
    hidden_wide, first_pull = jax.vjp(root_mean_scale, rows_wide, gain_first)
    hidden = hidden_wide.astype(bf16)
    key_pre = dot(hidden, w_key)
    values = dot(hidden, w_value).astype(bf16)
    query_pre = dot(hidden, w_query)
    key_gain_row = key_scale.reshape(1, HEAD_SIZE)
    query_gain_col = jnp.broadcast_to(query_scale[:, None], (HEAD_SIZE, 128))
    key_rot, prompt_keys, prompt_values = gather_keys(key_pre, values, key_gain_row, cos_rows, sin_rows, rows, n, 2)
    attended, query_rot, lse, query_rs = attend(
        query_pre, prompt_keys, prompt_values, key_rot, values, query_gain_col, cos_t, sin_t, past, inside, rows
    )
    residual = rows_wide + dot(attended, w_out)
    hidden_two_wide, second_pull = jax.vjp(root_mean_scale, residual, gain_second)
    hidden_two = hidden_two_wide.astype(bf16)
    gate_pre = dot(hidden_two, w_gate)
    up_pre = dot(hidden_two, w_up)
    act_wide, act_pull = jax.vjp(swiglu, gate_pre, up_pre)
    act = act_wide.astype(bf16)
    mixed_full = residual + dot(act, w_down)
    d_mixed = jnp.concatenate([prompt_cotangent, moved_cotangent], 0).astype(f32) * valid_rows[:, None]
    d_mixed_low = d_mixed.astype(bf16)
    grad_down = dot_tn(act, d_mixed_low).astype(bf16)
    d_act = dot_nt(d_mixed_low, w_down)
    d_gate_wide, d_up_wide = act_pull(d_act)
    d_gate, d_up = d_gate_wide.astype(bf16), d_up_wide.astype(bf16)
    grad_gate = dot_tn(hidden_two, d_gate).astype(bf16)
    grad_up = dot_tn(hidden_two, d_up).astype(bf16)
    d_hidden_two = dot_nt(d_gate, w_gate) + dot_nt(d_up, w_up)
    d_resid_mlp, grad_second_gain = second_pull(d_hidden_two)
    d_resid = d_mixed + d_resid_mlp
    d_resid_low = d_resid.astype(bf16)
    grad_out = dot_tn(attended, d_resid_low).astype(bf16)
    d_attended = dot_nt(d_resid_low, w_out).astype(bf16)
    d_query, dk, dv, dk_own, dv_own, gain_part = attend_back(
        query_rot, prompt_keys, prompt_values, key_rot, values, d_attended, attended, lse, query_rs, query_gain_col, cos_t, sin_t, past, inside, rows
    )
    grad_query_gain = jnp.sum(gain_part, axis=1)
    d_key, d_value, key_gain_part = key_grads(dk, dv, dk_own, dv_own, key_pre, key_gain_row, cos_rows, sin_rows, rows, n, 3)
    grad_key_gain = key_gain_part[0]
    grad_query = dot_tn(hidden, d_query).astype(bf16)
    grad_key = dot_tn(hidden, d_key).astype(bf16)
    grad_value = dot_tn(hidden, d_value).astype(bf16)
    d_hidden = dot_nt(d_query, w_query) + dot_nt(d_key, w_key) + dot_nt(d_value, w_value)
    d_rows_attn, grad_first_gain = first_pull(d_hidden)
    d_rows = d_resid + d_rows_attn
    stats = jnp.stack(
        [
            jnp.sum(valid_rows * jnp.sum(mixed_full * mixed_full, axis=-1)),
            jnp.sum(valid_rows * jnp.sum(residual * residual, axis=-1)),
            jnp.sum(valid_rows * jnp.sum(d_rows * d_rows, axis=-1)),
            jnp.sum(valid_rows),
        ]
    )
    vec = jnp.concatenate([grad_first_gain, grad_second_gain, grad_query_gain, grad_key_gain, jnp.pad(stats, (0, 124))])
    vec = jnp.pad(vec.reshape(-1, 128), ((0, (-vec.shape[0] // 128) % 8), (0, 0)))
    mixed_low = mixed_full.astype(bf16)
    back = spread([cut(mixed_low[rows:]), cut(d_rows[rows:].astype(bf16))], n, 4)
    shards, vec_sum = scatter([grad_down, grad_gate, grad_up, grad_out, grad_query, grad_key, grad_value], n, R, 5, vec)
    suffix_mixed, suffix_grad = [v.reshape(suffix, width) for v in collect(place, back, n, 6)]
    g_down, g_gate, g_up, g_out, g_query, g_key, g_value = [g.astype(f32) for g in shards]
    flat = vec_sum.reshape(-1)

    def mine(first, size, part):
        return lax.dynamic_slice_in_dim(flat[first : first + size], rank * part, part)

    g_first = mine(0, width, attention_gain.size)
    g_second = mine(width, width, mlp_gain.size)
    g_query_gain = mine(2 * width, HEAD_SIZE, query_gain.size)
    g_key_gain = mine(2 * width + HEAD_SIZE, HEAD_SIZE, key_norm_gain.size)
    stat_sums = flat[2 * width + 2 * HEAD_SIZE : 2 * width + 2 * HEAD_SIZE + 4]
    token_norms = jnp.sqrt(stat_sums[:3] / (stat_sums[3] * width))
    return (
        mixed_low[:rows],
        suffix_mixed,
        d_rows[:rows],
        suffix_grad.astype(f32),
        g_first,
        g_query,
        g_key,
        g_value,
        g_query_gain,
        g_key_gain,
        g_out,
        g_second,
        g_gate,
        g_up,
        g_down,
        token_norms,
    )


def solution(mesh):
    placed = (
        P(("rep", "fsdp"), None),
        P(("rep", "fsdp"), None),
        P("rep", "fsdp"),
        P("rep", "fsdp"),
        P("fsdp"),
        P("fsdp", None),
        P("fsdp", None),
        P("fsdp", None),
        P("fsdp"),
        P("fsdp"),
        P("fsdp", None),
        P("fsdp"),
        P("fsdp", None),
        P("fsdp", None),
        P("fsdp", None),
        P(("rep", "fsdp"), None),
        P(("rep", "fsdp"), None),
    )
    return jax.shard_map(
        per_device,
        mesh=mesh,
        in_specs=placed,
        out_specs=(
            P(("rep", "fsdp"), None),
            P(("rep", "fsdp"), None),
            P(("rep", "fsdp"), None),
            P(("rep", "fsdp"), None),
            P("fsdp"),
            P("fsdp", None),
            P("fsdp", None),
            P("fsdp", None),
            P("fsdp"),
            P("fsdp"),
            P("fsdp", None),
            P("fsdp"),
            P("fsdp", None),
            P("fsdp", None),
            P("fsdp", None),
            P(),
        ),
        check_vma=False,
    )
```

time: 1150 us -> 739 us (0.64)
  waiting for transfers between devices: 272 us -> 0 us
  Pallas kernels: 342 us -> 581 us
  local copies, waits for them, and re-layouts: 231 us -> 13.9 us
  matrix products: 176 us -> 107 us
  other arithmetic: 95.2 us -> 28.9 us
  between operations: 16 us -> 2.21 us
    pallas_call x1 -> x8, Pallas kernels: 173 us -> 410 us  [the longest x1 204 us: gather(): pl.pallas_call(partial(gather_kernel, n, m, k), out_shape=outs, in_specs=...]
    reduce_scatter x2 -> x0, waiting for transfers between devices: 142 us -> none  [the longest x1 99.5 us: per_device(): lax.psum_scatter(key_buffer.astype(jnp.bfloat16), 'fsdp', scatter_dimensi...]
    all_gather x2 -> x0, waiting for transfers between devices: 129 us -> none  [the longest x1 67 us: per_device(): lax.all_gather(value_matrix_rows[:prompt_on_device], 'fsdp', axis=0, tile...]
    dynamic_update_slice x6 -> x0, local copies, waits for them, and re-layouts: 84.7 us -> none  [the longest x2 53.2 us: per_device(): lax.map(slot_forward, (slot_query_rows, slot_key_rows, slot_value_rows, o...]
    dot_general x41 -> x21, matrix products: 176 us -> 107 us  [the longest x7 38.5 us: dot(): return jnp.dot(x, y, preferred_element_type=f32)]
    unnamed x181 -> x101, local copies, waits for them, and re-layouts: 42.4 us -> 4.12 us
    dynamic_slice x32 -> x5, local copies, waits for them, and re-layouts: 31.6 us -> 2.41 us  [the longest x4 2.33 us: mine(): return lax.dynamic_slice_in_dim(flat[first:first + size], rank * part, part)]
    dynamic_update_slice x4 -> x0, other arithmetic: 24.3 us -> none  [the longest x2 24.2 us: slot_backward(): lax.dynamic_update_slice_in_dim(value_acc, lax.dynamic_slice_in_dim(value...]
  transfers between devices with their start and end apart: 4 -> 0, of which waited for: 4 -> 0; matrix products, arithmetic and copies ran while one was open for 9% -> 0% of each run, Pallas kernels for 0% -> 0%
where the time goes in v2:
time: 739 us; the launch traced here: 733 us
  Pallas kernels  581 us (79%)
  matrix products  107 us (14%)
  other arithmetic  28.9 us (4%)
  local copies, waits for them, and re-layouts  13.9 us (2%)
    pallas_call x1, Pallas kernels, gather(): pl.pallas_call(partial(gather_kernel, n, m, k), out_shape=outs, in_specs=...  204 us
    pallas_call x1, Pallas kernels, scatter(): pl.pallas_call(partial(scatter_kernel, n, R, m, vec is not None), out_sha...  171 us
    pallas_call x2, Pallas kernels, collect(): pl.pallas_call(partial(collect_kernel, n, k), out_shape=[jax.ShapeDtypeSt...  61.7 us
    dot_general x7, matrix products, dot(): return jnp.dot(x, y, preferred_element_type=f32)  38.5 us
    dot_general x7, matrix products, dot_nt(): return jnp.einsum('ra,ba->rb', x, y, preferred_element_type=f32)  36.2 us
    pallas_call x1, Pallas kernels, key_grads(): pl.pallas_call(partial(key_grads_kernel, n, group), out_shape=[jax.ShapeD...  35.4 us
    pallas_call x1, Pallas kernels, gather_keys(): pl.pallas_call(partial(keys_kernel, n, group), out_shape=[jax.ShapeDtypeS...  32.7 us
    dot_general x7, matrix products, dot_tn(): return jnp.einsum('ra,rb->ab', x, y, preferred_element_type=f32)  32.5 us

profile of v2, /device:TPU:0, one launch (start us, length us, event | category | flops | bytes accessed | tf_op | source)
XLA Modules:
  0.0 733.2 jit_solution(8902366708947200279)
XLA Ops:
  4.2 204.4 %gather.1 = (bf16[4,2,2,2,2,16,1024]{6,5,4,3,2,1,0:T(8,128)(2,1)}, bf16[4,2,2,2,2,16,1024]{6,5,4,3,2,1,0:T(8,128)(2,1)}, bf16[4,2,2,2,2,16,2048]{6,5,4,3,2,1,0:T...) custom-call(bf16[2,2,16,1024]{3,2,1,0:T(8,128)(2,1)} %bitcast.171, ...), custom_call_target="tpu_custom_call" | custom-call | tf_op jit(solution)/shard_map/gather/pallas_call | solution.py:140
  210.6 33.2 %collect.2 = (bf16[2,16,8,1024]{3,2,1,0:T(8,128)(2,1)}, bf16[2,16,8,1024]{3,2,1,0:T(8,128)(2,1)}) custom-call(s32[32]{0:T(128)} %get-tuple-element.111.refs_0_, bf16[32,8,1024]{2,1,0:T(8,128)(2,1)} %bitcast.160, bf16[32,8,1024]{2,1,0:T(8,128)(2,1)} %bitcast.161), custom_call_target="tpu_custom_call" | custom-call | tf_op jit(solution)/shard_map/collect/pallas_call | solution.py:228
  245.4 4.2 convolution_convert_fusion.8.v.v_own
  249.5 2.7 fusion.32.k_pre
  252.9 32.7 %prompt_keys.1 = (bf16[512,1024]{1,0:T(8,128)(2,1)}, bf16[2,2,256,1024]{3,2,1,0:T(8,128)(2,1)}, bf16[2,2,256,1024]{3,2,1,0:T(8,128)(2,1)}) custom-call(f32[512,1024]{1,0:T(8,128)} %fusion.32.k_pre, bf16[512,1024]{1,0:T(8,128)(2,1)} %convolution_convert_fusion.8.v.v_own, f32[1,128]{1,0:T(1,128)} %reshape_reshape_squeeze.3.gain, ...), custom_call_target="tpu_custom_call" | custom-call | tf_op jit(solution)/shard_map/prompt_keys/pallas_call | solution.py:443
  286.9 6.6 fusion.34.q_pre
  296.4 20.2 %attend.1 = (bf16[512,2048]{1,0:T(8,128)(2,1)}, bf16[2048,512]{1,0:T(8,128)(2,1)}, f32[8,2,512]{2,1,0:T(2,128)}, f32[8,2,512]{2,1,0:T(2,128)}) custom-call(f32[512,2048]{1,0:T(8,128)} %fusion.34.q_pre, bf16[1024,1024]{1,0:T(8,128)(2,1)} %bitcast.131, bf16[1024,1024]{1,0:T(8,128)(2,1)} %bitcast.133, bf16[512,1024]{1,0:T(8,128)(2,1)} %get-tuple-element.65.k_own, ...), custom_call_target="tpu_custom_call" | custom-call | tf_op jit(solution)/shard_map/attend/pallas_call | solution.py:572
  316.6 5.3 multiply_reduce_fusion.4
  322.2 9.4 %fusion.40 = f32[512,3072]{1,0:T(8,128)} fusion(bf16[512,1024]{1,0:T(8,128)(2,1)S(1)} %multiply_convert_fusion.2, bf16[1024,3072]{1,0:T(8,128)(2,1)} %bitcast.182), kind=kOutput, calls=%fused_computation.136 | convolution fusion | flops 3221225472 | bytes 13631488 | tf_op jit(solution)/shard_map/dot_general | solution.py:676
  331.7 5.8 fusion.39
  337.6 11.2 %multiply_convert_fusion = (bf16[512,3072]{1,0:T(8,128)(2,1)S(1)}, bf16[512,3072]{1,0:T(8,128)(2,1)}, bf16[512,3072]{1,0:T(8,128)(2,1)}) fusion(f32[512,3072]{1,0:T(8,128)} %fusion.39, f32[512,3072]{1,0:T(8,128)} %fusion.40, bf16[3072,1024]{1,0:T(8,128)(2,1)S(1)} %bitcast.178, f32[512]{0:T(512)S(1)} %pad_convert_fusion, bf16[256,1024]{1,0:T(8,128)(2,1)S(1)} %bitcast.156, ...), kind=kOutput, calls=%fused_computation.4 | convolution fusion | flops 3249537024 | bytes 29362176 | tf_op jit(solution)/shard_map/ra,ba->rb/dot_general | solution.py:684
  348.7 7.7 %fusion.41 = f32[512,1024]{1,0:T(8,128)S(1)} fusion(bf16[512,3072]{1,0:T(8,128)(2,1)} %get-tuple-element.115, bf16[1024,3072]{1,0:T(8,128)(2,1)} %bitcast.184), kind=kOutput, calls=%fused_computation.137 | convolution fusion | flops 3221225472 | bytes 11534336 | tf_op jit(solution)/shard_map/ra,ba->rb/dot_general | solution.py:684
  356.4 6.0 multiply_reduce_fusion.2
  362.4 2.4 fusion.8
  365.3 3.8 convolution_convert_fusion.5.d_out
  369.0 30.4 %attend_back.1 = (bf16[512,2048]{1,0:T(8,128)(2,1)}, bf16[1024,1024]{1,0:T(8,128)(2,1)}, bf16[1024,1024]{1,0:T(8,128)(2,1)}, bf16[256,1024]{1,0:T(8,128)(2,1)}, ...) custom-call(bf16[2048,512]{1,0:T(8,128)(2,1)} %get-tuple-element.72.q_rot, bf16[1024,1024]{1,0:T(8,128)(2,1)} %bitcast.132, ...), custom_call_target="tpu_custom_call" | custom-call | tf_op jit(solution)/shard_map/attend_back/pallas_call | solution.py:650
  399.4 35.4 %prompt_key_grads.1 = (bf16[512,1024]{1,0:T(8,128)(2,1)}, bf16[512,1024]{1,0:T(8,128)(2,1)}, f32[8,128]{1,0:T(8,128)}) custom-call(bf16[2,2,256,1024]{3,2,1,0:T(8,128)(2,1)} %bitcast.154, bf16[2,2,256,1024]{3,2,1,0:T(8,128)(2,1)} %bitcast.155, bf16[256,1024]{1,0:T(8,128)(2,1)} %get-tuple-element.78.dks, bf16[256,1024]{1,0:T(8,128)(2,1)} %get-tuple-element.79.dvs, ...), custom_call_target="tpu_custom_call" | custom-call | tf_op jit(solution)/shard_map/prompt_key_grads/pallas_call | solution.py:530
  434.8 3.3 fusion.42
  440.4 3.0 fusion.7
  446.7 4.5 multiply_reduce_fusion.1
  452.6 2.7 constant_dynamic-update-slice_fusion
  455.9 4.0 convolution_convert_fusion.6
  459.9 2.7 convolution_convert_fusion.7
  462.6 4.7 convolution_convert_fusion.3
  467.4 4.4 convolution_convert_fusion.4
  471.8 5.6 convolution_convert_fusion
  477.4 5.4 convolution_convert_fusion.1
  482.8 5.7 convolution_convert_fusion.2
  488.5 171.3 %scatter.1 = (bf16[2,2,48,1024]{3,2,1,0:T(8,128)(2,1)}, bf16[2,2,16,3072]{3,2,1,0:T(8,128)(2,1)}, bf16[2,2,16,3072]{3,2,1,0:T(8,128)(2,1)}, bf16[2,2,32,1024]{3,...) custom-call(bf16[4,2,2,2,2,48,1024]{6,5,4,3,2,1,0:T(8,128)(2,1)} %bi, ...), custom_call_target="tpu_custom_call" | custom-call | tf_op jit(solution)/shard_map/scatter/pallas_call | solution.py:368
  675.5 24.9 %spread.1 = (bf16[16,2,8,1024]{3,2,1,0:T(8,128)(2,1)}, bf16[16,2,8,1024]{3,2,1,0:T(8,128)(2,1)}) custom-call(bf16[2,16,8,1024]{3,2,1,0:T(8,128)(2,1)} %bitcast.153, bf16[2,16,8,1024]{3,2,1,0:T(8,128)(2,1)} %bitcast.152), custom_call_target="tpu_custom_call" | custom-call | tf_op jit(solution)/shard_map/spread/pallas_call | solution.py:181
  700.4 28.5 %collect.3 = (bf16[2,16,8,1024]{3,2,1,0:T(8,128)(2,1)}, bf16[2,16,8,1024]{3,2,1,0:T(8,128)(2,1)}) custom-call(s32[32]{0:T(128)} %copy-done.22, bf16[32,8,1024]{2,1,0:T(8,128)(2,1)} %bitcast.162, bf16[32,8,1024]{2,1,0:T(8,128)(2,1)} %bitcast.163), custom_call_target="tpu_custom_call" | custom-call | tf_op jit(solution)/shard_map/collect/pallas_call | solution.py:228
  728.9 2.2 bitcast_convert_fusion
  (166 shorter events, 36.8 us)
Async XLA Ops:
  3.5 240.4 %copy-start.4 = (bf16[256,1024]{1,0:T(8,128)(2,1)S(1)}, bf16[256,1024]{1,0:T(8,128)(2,1)}, u32[]{:S(2)}) copy-start(bf16[256,1024]{1,0:T(8,128)(2,1)} %param.17) | copy-start | bytes 1572868
  208.6 36.6 %copy-start.20 = (f32[16,8,128]{2,1,0:T(8,128)S(1)}, f32[16,8,128]{2,1,0:T(8,128)}, u32[]{:S(2)}) copy-start(f32[16,8,128]{2,1,0:T(8,128)} %get-tuple-element.56) | copy-start | bytes 196612
  209.9 39.6 %copy-start.22 = (s32[32]{0:T(128)}, s32[32]{0:T(128)S(1)}, u32[]{:S(2)}) copy-start(s32[32]{0:T(128)S(1)} %convert_reduce_fusion.refs_0_) | copy-start | bytes 388
  245.4 4.2 copy-start.30
  321.9 34.5 %copy-start = (f32[512,1024]{1,0:T(8,128)}, f32[512,1024]{1,0:T(8,128)S(1)}, u32[]{:S(2)}) copy-start(f32[512,1024]{1,0:T(8,128)S(1)} %get-tuple-element.131) | copy-start | bytes 6291460
  322.0 9.7 %slice-start.4 = ((s8[6291456]{0:T(1024)(128)(4,1)}), s8[4194304]{0:T(1024)(128)(4,1)S(1)}, s32[]{:S(2)}) async-start(s8[6291456]{0:T(1024)(128)(4,1)} %bitcast.185), calls=%async_computation.4 | async-start | bytes 8388608
  322.2 9.4 %copy-start.7 = (bf16[512,1024]{1,0:T(8,128)(2,1)}, bf16[512,1024]{1,0:T(8,128)(2,1)S(1)}, u32[]{:S(2)}) copy-start(bf16[512,1024]{1,0:T(8,128)(2,1)S(1)} %multiply_convert_fusion.2) | copy-start | bytes 3145732
  322.2 9.4 %slice-start.5 = ((s8[6291456]{0:T(1024)(128)(4,1)}), s8[2097152]{0:T(1024)(128)(4,1)S(1)}, s32[]{:S(2)}) async-start(s8[6291456]{0:T(1024)(128)(4,1)} %bitcast.185), calls=%async_computation.5 | async-start | bytes 4194304
  322.2 15.3 %slice-start = ((s8[6291456]{0:T(1024)(128)(4,1)}), s8[4194304]{0:T(1024)(128)(4,1)S(1)}, s32[]{:S(2)}) async-start(s8[6291456]{0:T(1024)(128)(4,1)} %bitcast.176), calls=%async_computation | async-start | bytes 8388608
  331.7 5.9 copy-start.9
  331.7 5.9 copy-start.11
  331.7 5.9 slice-start.1
  348.7 7.7 %copy-start.37 = (bf16[512,3072]{1,0:T(8,128)(2,1)}, bf16[512,3072]{1,0:T(8,128)(2,1)S(1)}, u32[]{:S(2)}) copy-start(bf16[512,3072]{1,0:T(8,128)(2,1)S(1)} %get-tuple-element.114) | copy-start | bytes 9437188
  434.8 4.7 copy-start.31
  438.2 7.4 %slice-start.2 = ((s8[6291456]{0:T(1024)(128)(4,1)}), s8[4194304]{0:T(1024)(128)(4,1)S(1)}, s32[]{:S(2)}) async-start(s8[6291456]{0:T(1024)(128)(4,1)} %bitcast.179), calls=%async_computation.2 | async-start | bytes 8388608
  440.4 5.2 slice-start.3
  446.7 5.1 copy-start.19
  462.6 4.8 copy-start.3
  467.4 4.4 copy-start.8
  467.4 4.4 copy-start.38
  471.8 5.6 copy-start.39
  477.4 5.4 copy-start.10
  477.4 5.4 copy-start.12
  477.4 5.4 copy-start.41
  659.8 7.3 copy-start.14
  659.8 8.3 %copy-start.16 = (bf16[2,2,32,1024]{3,2,1,0:T(8,128)(2,1)S(1)}, bf16[2,2,32,1024]{3,2,1,0:T(8,128)(2,1)}, u32[]{:S(2)}) copy-start(bf16[2,2,32,1024]{3,2,1,0:T(8,128)(2,1)} %get-tuple-element.92) | copy-start | bytes 786436
  663.0 5.9 copy-start.15
  665.0 4.8 copy-start.18
  665.0 5.5 copy-start.17
  665.0 6.2 copy-start.21
  665.0 8.6 %copy-start.2 = (f32[512,1024]{1,0:T(8,128)S(1)}, f32[512,1024]{1,0:T(8,128)}, u32[]{:S(2)}) copy-start(f32[512,1024]{1,0:T(8,128)} %get-tuple-element.113) | copy-start | bytes 6291460
  667.1 7.4 %copy-start.6 = (bf16[512,1024]{1,0:T(8,128)(2,1)S(1)}, bf16[512,1024]{1,0:T(8,128)(2,1)}, u32[]{:S(2)}) copy-start(bf16[512,1024]{1,0:T(8,128)(2,1)} %get-tuple-element.118) | copy-start | bytes 3145732
  (16 other events, 48.3 us)
